TPU v7x, 256 devices: a whole 4x4x8 slice. The times are simulated.
256 devices in a mesh: rows: 16 (over y_lo, z), cols: 8 (over x, y_hi), dp: 2 (over core).
Axes of the slice: x: 4, y: 4 (y_hi: 2, y_lo: 2; y = y_hi * 2 + y_lo), z: 8, core: 2. Of those that a mesh axis runs over, the one named last changes fastest.
Arguments:
- features: bfloat16 [2, 32, 512, 2048], P('dp', None, 'rows', 'cols'), may hold values from -6 to 6
- shifts: int32 [2, 32, 2], P('dp'), may hold values from -16 to 16, as said below
- first_kernel: bfloat16 [9, 32, 32], replicated, may hold values from -0.375 to 0.375
- bottle_kernel: bfloat16 [9, 32, 32], replicated, may hold values from -0.375 to 0.375
- second_kernel: bfloat16 [9, 32, 32], replicated, may hold values from -0.375 to 0.375
- cotangent: bfloat16 [2, 32, 512, 2048], P('dp', None, 'rows', 'cols'), may hold values from -6 to 6
Outputs:
- prediction: bfloat16 [2, 32, 512, 2048], P('dp', None, 'rows', 'cols')
- first_grad: float32 [9, 32, 32], replicated
- second_grad: float32 [9, 32, 32], replicated
Inputs may be any that keep to these rules, and one draw needn't show every extreme that they name: `shifts`: every image has one channel displaced by exactly 16 and another by exactly -16 along one direction.
All inputs are finite; a program needn't handle non-finite values.
Results may differ from a plain program's by a relative error of at most 0.0059.
Values may be sent and summed in bfloat16 or wider, within the bound.
A program may use at most 64 MiB of HBM per device.

v0:
```python
import math

import jax
import jax.numpy as jnp
from jax import lax
from jax.sharding import PartitionSpec as P

MAXSHIFT = 16
POOL = 4


def padded(block, sides, width):
    for axis, dim in sides:
        count = lax.axis_size(axis)
        forward = [(i, i + 1) for i in range(count - 1)]
        backward = [(target, source) for source, target in forward]
        low = lax.ppermute(
            lax.slice_in_dim(block, block.shape[dim] - width, None, axis=dim), axis, forward
        )
        high = lax.ppermute(lax.slice_in_dim(block, 0, width, axis=dim), axis, backward)
        block = jnp.concatenate([low, block, high], axis=dim)
    return block


def stored(values):
    return lax.optimization_barrier(values.astype(jnp.bfloat16))


def convolve_ext(extended, kernel, transpose):
    height = extended.shape[2] - 2
    span = extended.shape[3] - 2
    result = None
    for tap_index in range(9):
        row_off = tap_index // 3 - 1
        col_off = tap_index % 3 - 1
        if transpose:
            window = extended[
                :, :, 1 - row_off : 1 - row_off + height, 1 - col_off : 1 - col_off + span
            ]
            term = jnp.einsum(
                "oi,bohw->bihw", kernel[tap_index], window, preferred_element_type=jnp.float32
            )
        else:
            window = extended[
                :, :, 1 + row_off : 1 + row_off + height, 1 + col_off : 1 + col_off + span
            ]
            term = jnp.einsum(
                "oi,bihw->bohw", kernel[tap_index], window, preferred_element_type=jnp.float32
            )
        result = term if result is None else result + term
    return result


def correlate(grad_out, extended):
    height = grad_out.shape[2]
    span = grad_out.shape[3]
    pieces = []
    for tap_index in range(9):
        row_off = tap_index // 3 - 1
        col_off = tap_index % 3 - 1
        window = extended[
            :, :, 1 + row_off : 1 + row_off + height, 1 + col_off : 1 + col_off + span
        ]
        pieces.append(
            jnp.einsum("bohw,bihw->oi", grad_out, window, preferred_element_type=jnp.float32)
        )
    return jnp.stack(pieces)


def pool_sum(values):
    shape = values.shape
    return values.reshape(shape[0], shape[1], shape[2] // POOL, POOL, shape[3] // POOL, POOL).sum(
        axis=(3, 5)
    )


def upsample(values):
    return jnp.repeat(jnp.repeat(values, POOL, axis=2), POOL, axis=3)


def warp_planes(rimmed, shifts, margin_in, margin_out, height, span):

    def single_plane(channel_plane, row_shift, col_shift):
        return lax.dynamic_slice(
            channel_plane,
            (margin_in - margin_out + row_shift, margin_in - margin_out + col_shift),
            (height + 2 * margin_out, span + 2 * margin_out),
        )

    return jax.vmap(jax.vmap(single_plane))(rimmed, shifts[..., 0], shifts[..., 1])


def coarse_conv(coarse_in, kernel, transpose):
    extended = padded(coarse_in, (("rows", 2), ("cols", 3)), 1)
    return convolve_ext(extended, kernel, transpose)


def shards(features, shifts, first_kernel, bottle_kernel, second_kernel, cotangent):
    height = features.shape[2]
    span = features.shape[3]
    rimmed = padded(features, (("rows", 2), ("cols", 3)), MAXSHIFT)
    warped = warp_planes(rimmed, shifts, MAXSHIFT, 0, height, span)
    warped_ext = padded(warped, (("rows", 2), ("cols", 3)), 1)
    first_pre = convolve_ext(warped_ext, first_kernel, False)
    first_act = stored(jax.nn.silu(first_pre))
    pooled = stored(pool_sum(first_act.astype(jnp.float32)) / (POOL * POOL))
    bottle = coarse_conv(pooled, bottle_kernel, False)
    blended = stored(first_act.astype(jnp.float32) + upsample(bottle))
    blended_ext = padded(blended, (("rows", 2), ("cols", 3)), 1)
    cotangent_ext = padded(cotangent, (("rows", 2), ("cols", 3)), 1)
    prediction = convolve_ext(blended_ext, second_kernel, False).astype(jnp.bfloat16)
    factor = 1.0 / math.sqrt(
        features.shape[0]
        * lax.axis_size("dp")
        * height
        * lax.axis_size("rows")
        * span
        * lax.axis_size("cols")
    )
    second_grad = correlate(cotangent, blended_ext) * factor
    blend_grad = stored(convolve_ext(cotangent_ext, second_kernel, True))
    coarse_grad = stored(pool_sum(blend_grad.astype(jnp.float32)))
    pooled_grad = coarse_conv(coarse_grad, bottle_kernel, True)
    act_grad = blend_grad.astype(jnp.float32) + upsample(pooled_grad) / (POOL * POOL)
    sigma = jax.nn.sigmoid(first_pre)
    pre_grad = (act_grad * sigma * (1.0 + first_pre * (1.0 - sigma))).astype(jnp.bfloat16)
    first_grad = correlate(pre_grad, warped_ext) * factor
    first_grad, second_grad = lax.psum((first_grad, second_grad), ("rows", "cols", "dp"))
    return (prediction, first_grad, second_grad)


def solution(mesh):
    placed = (
        P("dp", None, "rows", "cols"),
        P("dp", None, None),
        P(),
        P(),
        P(),
        P("dp", None, "rows", "cols"),
    )
    return jax.shard_map(
        shards,
        mesh=mesh,
        in_specs=placed,
        out_specs=(P("dp", None, "rows", "cols"), P(), P()),
        check_vma=False,
    )
```

profile of v0, /device:TPU:1, one launch (start us, length us, event | category | flops | bytes accessed | tf_op | source)
XLA Modules:
  0.0 596.3 jit_solution(9801430774848954022)
XLA Ops:
  8.6 4.5 collective-permute-start.16
  16.3 4.9 collective-permute-start
  23.0 4.8 collective-permute-start.19
  29.9 12.0 %collective-permute-done.18 = bf16[1,32,34,1]{3,1,2,0:T(8,128)(2,1)S(1)} collective-permute-done((bf16[1,32,34,1]{3,1,2,0:T(8,128)(2,1)S(1)}, bf16[1,32,34,1]{3,1,2,0:T(8,128)(2,1)S(1)}, u32[]{:S(2)}, u32[]{:S(2)}) %collective-permute-start.18) | collective-permute-done | bytes 2208 | tf_op jit(solution)/shard_map/ppermute | solution.py:20
  42.3 1.9 collective-permute-done.19
  46.7 2.4 copy.180
  49.1 3.6 reduce_sum.19
  54.2 4.0 collective-permute-start.20
  60.5 6.2 %collective-permute-start.23 = (bf16[1,32,10,1]{3,1,2,0:T(8,128)(2,1)S(1)}, bf16[1,32,10,1]{3,1,2,0:T(8,128)(2,1)S(1)}, u32[]{:S(2)}, u32[]{:S(2)}) collective-permute-start(bf16[1,32,10,1]{3,1,2,0:T(8,128)(2,1)S(1)} %get-tuple-element.61), channel_id=1, source_target_pairs={{0,2},{2,4},{4,6},{6,8},{8,10},{10,12},{12,14},{1,3},{3,5},{5,7},{... | collective-permute-start | bytes 1928 | tf_op jit(solution)/shard_map/ppermute | solution.py:17
  73.3 6.5 %collective-permute-start.2 = (bf16[1,32,64,16]{3,2,1,0:T(8,128)(2,1)S(1)}, bf16[1,32,64,16]{3,2,1,0:T(8,128)(2,1)S(1)}, u32[]{:S(2)}, u32[]{:S(2)}) collective-permute-start(bf16[1,32,64,16]{3,2,1,0:T(8,128)(2,1)S(1)} %get-tuple-element.38), channel_id=1, source_target_pairs={{0,2},{2,4},{4,6},{6,8},{8,10},{10,12},{12,14},{1,3},{3,5},{5,7},{... | collective-permute-start | bytes 196616 | tf_op jit(solution)/shard_map/ppermute | solution.py:17
  80.0 7.4 %collective-permute-done.3 = bf16[1,32,64,16]{3,2,1,0:T(8,128)(2,1)S(1)} collective-permute-done((bf16[1,32,64,16]{3,2,1,0:T(8,128)(2,1)S(1)}, bf16[1,32,64,16]{3,2,1,0:T(8,128)(2,1)S(1)}, u32[]{:S(2)}, u32[]{:S(2)}) %collective-permute-start.3) | collective-permute-done | bytes 65568 | tf_op jit(solution)/shard_map/ppermute | solution.py:20
  87.4 14.6 %collective-permute-done.2 = bf16[1,32,64,16]{3,2,1,0:T(8,128)(2,1)S(1)} collective-permute-done((bf16[1,32,64,16]{3,2,1,0:T(8,128)(2,1)S(1)}, bf16[1,32,64,16]{3,2,1,0:T(8,128)(2,1)S(1)}, u32[]{:S(2)}, u32[]{:S(2)}) %collective-permute-start.2) | collective-permute-done | bytes 65568 | tf_op jit(solution)/shard_map/ppermute | solution.py:17
  102.0 2.3 pad_maximum_fusion
  104.3 112.1 %while.1 = (s32[]{:T(128)}, bf16[1,32,64,288]{3,2,1,0:T(8,128)(2,1)}, s32[32,4]{0,1:T(4,128)S(1)}, bf16[32,32,256]{2,1,0:T(8,128)(2,1)S(1)}, s32[]{:T(128)}) while((s32[]{:T(128)}, bf16[1,32,64,288]{3,2,1,0:T(8,128)(2,1)}, s32[32,4]{0,1:T(4,128)S(1)}, bf16[32,32,256]{2,1,0:T(8,128)(2,1)S(1)}, s32[]{:T(128)}) %tuple.47), condition=%wide.while_cond, body=%wide.while_body.sunk | while | flops 2 | bytes 32913 | solution.py:84
  105.0 2.8 bitcast_dynamic-update-slice_fusion.2
  108.5 2.8 bitcast_dynamic-update-slice_fusion.2
  112.0 2.8 bitcast_dynamic-update-slice_fusion.2
  115.5 2.8 bitcast_dynamic-update-slice_fusion.2
  119.0 2.8 bitcast_dynamic-update-slice_fusion.2
  122.5 2.8 bitcast_dynamic-update-slice_fusion.2
  126.0 2.8 bitcast_dynamic-update-slice_fusion.2
  129.5 2.8 bitcast_dynamic-update-slice_fusion.2
  133.0 2.8 bitcast_dynamic-update-slice_fusion.2
  136.5 2.8 bitcast_dynamic-update-slice_fusion.2
  140.0 2.8 bitcast_dynamic-update-slice_fusion.2
  143.5 2.8 bitcast_dynamic-update-slice_fusion.2
  147.0 2.8 bitcast_dynamic-update-slice_fusion.2
  150.5 2.8 bitcast_dynamic-update-slice_fusion.2
  154.0 2.8 bitcast_dynamic-update-slice_fusion.2
  157.5 2.8 bitcast_dynamic-update-slice_fusion.2
  161.0 2.8 bitcast_dynamic-update-slice_fusion.2
  164.5 2.8 bitcast_dynamic-update-slice_fusion.2
  168.0 2.8 bitcast_dynamic-update-slice_fusion.2
  171.5 2.8 bitcast_dynamic-update-slice_fusion.2
  175.0 2.8 bitcast_dynamic-update-slice_fusion.2
  178.5 2.8 bitcast_dynamic-update-slice_fusion.2
  182.0 2.8 bitcast_dynamic-update-slice_fusion.2
  185.5 2.8 bitcast_dynamic-update-slice_fusion.2
  189.0 2.8 bitcast_dynamic-update-slice_fusion.2
  192.5 2.8 bitcast_dynamic-update-slice_fusion.2
  196.0 2.8 bitcast_dynamic-update-slice_fusion.2
  199.5 2.8 bitcast_dynamic-update-slice_fusion.2
  203.0 2.8 bitcast_dynamic-update-slice_fusion.2
  206.5 2.8 bitcast_dynamic-update-slice_fusion.2
  210.0 2.8 bitcast_dynamic-update-slice_fusion.2
  213.5 2.8 bitcast_dynamic-update-slice_fusion.2
  218.0 4.4 collective-permute-start.4
  223.6 2.5 broadcast_in_dim.23
  226.2 4.7 copy.192
  231.1 5.6 collective-permute-start.6
  238.4 3.6 collective-permute-done.6
  242.0 5.4 collective-permute-done.7
  253.6 3.3 copy.161
  256.9 3.6 reduce_sum.18
  262.1 4.0 collective-permute-start.8
  271.0 4.1 collective-permute-start.10
  276.8 8.1 %collective-permute-done.11 = bf16[1,32,10,1]{3,1,2,0:T(8,128)(2,1)S(1)} collective-permute-done((bf16[1,32,10,1]{3,1,2,0:T(8,128)(2,1)S(1)}, bf16[1,32,10,1]{3,1,2,0:T(8,128)(2,1)S(1)}, u32[]{:S(2)}, u32[]{:S(2)}) %collective-permute-start.11) | collective-permute-done | bytes 672 | tf_op jit(solution)/shard_map/ppermute | solution.py:20
  288.4 3.7 broadcast_in_dim.20
  292.1 4.8 copy.164
  299.7 4.0 collective-permute-start.12
  304.8 5.8 collective-permute-start.14
  312.1 2.1 collective-permute-done.14
  314.2 5.3 collective-permute-done.15
  331.1 255.2 %all-reduce.3.cloned.1.call-done = (f32[9,32,32]{2,1,0:T(8,128)}, f32[9,32,32]{2,1,0:T(8,128)}) async-done(((f32[9,32,32]{2,1,0:T(8,128)}, f32[9,32,32]{2,1,0:T(8,128)}), (f32[9,32,32]{2,1,0:T(8,128)}, f32[9,32,32]{2,1,0:T(8,128)})) %all-reduce.3.cloned.1.call-update) | async-done | bytes 73744 | tf_op jit(solution)/shard_map/psum | solution.py:128
  (231 shorter events, 85.6 us)
Async XLA Ops:
  7.2 15.4 %copy-start = (bf16[1,32,32,256]{3,2,1,0:T(8,128)(2,1)S(1)}, bf16[1,32,32,256]{3,2,1,0:T(8,128)(2,1)}, u32[]{:S(2)}) copy-start(bf16[1,32,32,256]{3,2,1,0:T(8,128)(2,1)} %param.11) | copy-start | bytes 1572868
  7.2 15.3 %copy-start.12 = (s32[1,32,2]{1,2,0:T(2,128)S(1)}, s32[1,32,2]{1,2,0:T(2,128)}, u32[]{:S(2)}) copy-start(s32[1,32,2]{1,2,0:T(2,128)} %param.7) | copy-start | bytes 772
  7.2 579.2 %all-reduce.3.cloned.1.call-start = ((), (), s32[]{:S(2)}) async-start(), calls=%async_computation | async-start | bytes 589824 | tf_op jit(solution)/shard_map/psum | solution.py:128
  8.6 20.5 %copy-start.7 = (bf16[9,32,32]{2,1,0:T(8,128)(2,1)S(1)}, bf16[9,32,32]{2,1,0:T(8,128)(2,1)}, u32[]{:S(2)}) copy-start(bf16[9,32,32]{2,1,0:T(8,128)(2,1)} %param.10) | copy-start | bytes 55300
  8.6 13.9 %collective-permute-start.16 = (bf16[1,32,1,256]{3,1,2,0:T(8,128)(2,1)S(1)}, bf16[1,32,1,256]{3,1,2,0:T(8,128)(2,1)S(1)}, u32[]{:S(2)}, u32[]{:S(2)}) collective-permute-start(bf16[1,32,1,256]{3,1,2,0:T(8,128)(2,1)S(1)} %get-tuple-element.51), channel_id=1, source_target_pairs={{0,16},{16,32},{32,48},{48,64},{64,80},{80,96},{96,112},{112,128},... | collective-permute-start | bytes 49160 | tf_op jit(solution)/shard_map/ppermute | solution.py:17
  13.1 9.7 %collective-permute-start.17 = (bf16[1,32,1,256]{3,1,2,0:T(8,128)(2,1)S(1)}, bf16[1,32,1,256]{3,1,2,0:T(8,128)(2,1)S(1)}, u32[]{:S(2)}, u32[]{:S(2)}) collective-permute-start(bf16[1,32,1,256]{3,1,2,0:T(8,128)(2,1)S(1)} %get-tuple-element.50), channel_id=1, source_target_pairs={{16,0},{32,16},{48,32},{64,48},{80,64},{96,80},{112,96},{128,112},... | collective-permute-start | bytes 49160 | tf_op jit(solution)/shard_map/ppermute | solution.py:20
  16.3 53.4 %collective-permute-start = (bf16[1,32,16,256]{3,2,1,0:T(8,128)(2,1)}, bf16[1,32,16,256]{3,2,1,0:T(8,128)(2,1)}, u32[]{:S(2)}, u32[]{:S(2)}) collective-permute-start(bf16[1,32,16,256]{3,2,1,0:T(8,128)(2,1)} %get-tuple-element.57), channel_id=1, source_target_pairs={{0,16},{16,32},{32,48},{48,64},{64,80},{80,96},{96,112},{112,128},... | collective-permute-start | bytes 786440 | tf_op jit(solution)/shard_map/ppermute | solution.py:17
  21.2 49.5 %collective-permute-start.1 = (bf16[1,32,16,256]{3,2,1,0:T(8,128)(2,1)}, bf16[1,32,16,256]{3,2,1,0:T(8,128)(2,1)}, u32[]{:S(2)}, u32[]{:S(2)}) collective-permute-start(bf16[1,32,16,256]{3,2,1,0:T(8,128)(2,1)} %get-tuple-element.56), channel_id=1, source_target_pairs={{16,0},{32,16},{48,32},{64,48},{80,64},{96,80},{112,96},{128,112},... | collective-permute-start | bytes 786440 | tf_op jit(solution)/shard_map/ppermute | solution.py:20
  23.0 21.2 %collective-permute-start.19 = (bf16[1,32,34,1]{3,1,2,0:T(8,128)(2,1)S(1)}, bf16[1,32,34,1]{3,1,2,0:T(8,128)(2,1)S(1)}, u32[]{:S(2)}, u32[]{:S(2)}) collective-permute-start(bf16[1,32,34,1]{3,1,2,0:T(8,128)(2,1)S(1)} %get-tuple-element.41), channel_id=1, source_target_pairs={{0,2},{2,4},{4,6},{6,8},{8,10},{10,12},{12,14},{1,3},{3,5},{5,7},{... | collective-permute-start | bytes 6536 | tf_op jit(solution)/shard_map/ppermute | solution.py:17
  27.9 14.0 %collective-permute-start.18 = (bf16[1,32,34,1]{3,1,2,0:T(8,128)(2,1)S(1)}, bf16[1,32,34,1]{3,1,2,0:T(8,128)(2,1)S(1)}, u32[]{:S(2)}, u32[]{:S(2)}) collective-permute-start(bf16[1,32,34,1]{3,1,2,0:T(8,128)(2,1)S(1)} %get-tuple-element.40), channel_id=1, source_target_pairs={{2,0},{4,2},{6,4},{8,6},{10,8},{12,10},{14,12},{3,1},{5,3},{7,5},{... | collective-permute-start | bytes 6536 | tf_op jit(solution)/shard_map/ppermute | solution.py:20
  49.1 17.6 %copy-start.8 = (bf16[9,32,32]{2,1,0:T(8,128)(2,1)S(1)}, bf16[9,32,32]{2,1,0:T(8,128)(2,1)}, u32[]{:S(2)}) copy-start(bf16[9,32,32]{2,1,0:T(8,128)(2,1)} %param.9) | copy-start | bytes 55300
  52.9 5.3 collective-permute-start.21
  54.2 4.8 collective-permute-start.20
  59.0 11.7 %copy-start.4 = (bf16[1,32,32,256]{3,2,1,0:T(8,128)(2,1)S(1)}, bf16[1,32,32,256]{3,2,1,0:T(8,128)(2,1)}, u32[]{:S(2)}) copy-start(bf16[1,32,32,256]{3,2,1,0:T(8,128)(2,1)} %param.6) | copy-start | bytes 1572868
  59.1 7.9 %collective-permute-start.22 = (bf16[1,32,10,1]{3,1,2,0:T(8,128)(2,1)S(1)}, bf16[1,32,10,1]{3,1,2,0:T(8,128)(2,1)S(1)}, u32[]{:S(2)}, u32[]{:S(2)}) collective-permute-start(bf16[1,32,10,1]{3,1,2,0:T(8,128)(2,1)S(1)} %get-tuple-element.60), channel_id=1, source_target_pairs={{2,0},{4,2},{6,4},{8,6},{10,8},{12,10},{14,12},{3,1},{5,3},{7,5},{... | collective-permute-start | bytes 1928 | tf_op jit(solution)/shard_map/ppermute | solution.py:20
  60.5 7.7 %collective-permute-start.23 = (bf16[1,32,10,1]{3,1,2,0:T(8,128)(2,1)S(1)}, bf16[1,32,10,1]{3,1,2,0:T(8,128)(2,1)S(1)}, u32[]{:S(2)}, u32[]{:S(2)}) collective-permute-start(bf16[1,32,10,1]{3,1,2,0:T(8,128)(2,1)S(1)} %get-tuple-element.61), channel_id=1, source_target_pairs={{0,2},{2,4},{4,6},{6,8},{8,10},{10,12},{12,14},{1,3},{3,5},{5,7},{... | collective-permute-start | bytes 1928 | tf_op jit(solution)/shard_map/ppermute | solution.py:17
  72.0 15.4 %collective-permute-start.3 = (bf16[1,32,64,16]{3,2,1,0:T(8,128)(2,1)S(1)}, bf16[1,32,64,16]{3,2,1,0:T(8,128)(2,1)S(1)}, u32[]{:S(2)}, u32[]{:S(2)}) collective-permute-start(bf16[1,32,64,16]{3,2,1,0:T(8,128)(2,1)S(1)} %get-tuple-element.39), channel_id=1, source_target_pairs={{2,0},{4,2},{6,4},{8,6},{10,8},{12,10},{14,12},{3,1},{5,3},{7,5},{... | collective-permute-start | bytes 196616 | tf_op jit(solution)/shard_map/ppermute | solution.py:20
  73.3 28.7 %collective-permute-start.2 = (bf16[1,32,64,16]{3,2,1,0:T(8,128)(2,1)S(1)}, bf16[1,32,64,16]{3,2,1,0:T(8,128)(2,1)S(1)}, u32[]{:S(2)}, u32[]{:S(2)}) collective-permute-start(bf16[1,32,64,16]{3,2,1,0:T(8,128)(2,1)S(1)} %get-tuple-element.38), channel_id=1, source_target_pairs={{0,2},{2,4},{4,6},{6,8},{8,10},{10,12},{12,14},{1,3},{3,5},{5,7},{... | collective-permute-start | bytes 196616 | tf_op jit(solution)/shard_map/ppermute | solution.py:17
  216.4 6.3 %copy-start.1 = (bf16[32,32,256]{2,1,0:T(8,128)(2,1)}, bf16[32,32,256]{2,1,0:T(8,128)(2,1)S(1)}, u32[]{:S(2)}) copy-start(bf16[32,32,256]{2,1,0:T(8,128)(2,1)S(1)} %get-tuple-element.10) | copy-start | bytes 1572868
  216.7 14.2 %collective-permute-start.5 = (bf16[1,32,1,256]{3,1,2,0:T(8,128)(2,1)S(1)}, bf16[1,32,1,256]{3,1,2,0:T(8,128)(2,1)S(1)}, u32[]{:S(2)}, u32[]{:S(2)}) collective-permute-start(bf16[1,32,1,256]{3,1,2,0:T(8,128)(2,1)S(1)} %get-tuple-element.55), channel_id=1, source_target_pairs={{16,0},{32,16},{48,32},{64,48},{80,64},{96,80},{112,96},{128,112},... | collective-permute-start | bytes 49160 | tf_op jit(solution)/shard_map/ppermute | solution.py:20
  218.0 12.9 %collective-permute-start.4 = (bf16[1,32,1,256]{3,1,2,0:T(8,128)(2,1)S(1)}, bf16[1,32,1,256]{3,1,2,0:T(8,128)(2,1)S(1)}, u32[]{:S(2)}, u32[]{:S(2)}) collective-permute-start(bf16[1,32,1,256]{3,1,2,0:T(8,128)(2,1)S(1)} %get-tuple-element.54), channel_id=1, source_target_pairs={{0,16},{16,32},{32,48},{48,64},{64,80},{80,96},{96,112},{112,128},... | collective-permute-start | bytes 49160 | tf_op jit(solution)/shard_map/ppermute | solution.py:17
  230.9 7.2 %copy-start.11 = (bf16[9,32,32]{2,1,0:T(8,128)(2,1)S(1)}, bf16[9,32,32]{2,1,0:T(8,128)(2,1)}, u32[]{:S(2)}) copy-start(bf16[9,32,32]{2,1,0:T(8,128)(2,1)} %param.8) | copy-start | bytes 55300
  230.9 20.1 %copy-start.9 = (bf16[1,32,1,256]{3,1,2,0:T(8,128)(2,1)}, bf16[1,32,1,256]{3,1,2,0:T(8,128)(2,1)S(1)}, u32[]{:S(2)}) copy-start(bf16[1,32,1,256]{3,1,2,0:T(8,128)(2,1)S(1)} %collective-permute-done.5) | copy-start | bytes 49156
  231.1 10.8 %collective-permute-start.6 = (bf16[1,32,34,1]{3,1,2,0:T(8,128)(2,1)S(1)}, bf16[1,32,34,1]{3,1,2,0:T(8,128)(2,1)S(1)}, u32[]{:S(2)}, u32[]{:S(2)}) collective-permute-start(bf16[1,32,34,1]{3,1,2,0:T(8,128)(2,1)S(1)} %get-tuple-element.48), channel_id=1, source_target_pairs={{0,2},{2,4},{4,6},{6,8},{8,10},{10,12},{12,14},{1,3},{3,5},{5,7},{... | collective-permute-start | bytes 6536 | tf_op jit(solution)/shard_map/ppermute | solution.py:17
  236.8 10.5 %collective-permute-start.7 = (bf16[1,32,34,1]{3,1,2,0:T(8,128)(2,1)S(1)}, bf16[1,32,34,1]{3,1,2,0:T(8,128)(2,1)S(1)}, u32[]{:S(2)}, u32[]{:S(2)}) collective-permute-start(bf16[1,32,34,1]{3,1,2,0:T(8,128)(2,1)S(1)} %get-tuple-element.49), channel_id=1, source_target_pairs={{2,0},{4,2},{6,4},{8,6},{10,8},{12,10},{14,12},{3,1},{5,3},{7,5},{... | collective-permute-start | bytes 6536 | tf_op jit(solution)/shard_map/ppermute | solution.py:20
  248.9 1.0 copy-start.2
  250.7 1.2 copy-start.6
  260.6 8.2 %copy-start.13 = (bf16[1,32,32,256]{3,1,2,0:T(8,128)(2,1)S(1)}, bf16[1,32,32,256]{3,1,2,0:T(8,128)(2,1)}, u32[]{:S(2)}) copy-start(bf16[1,32,32,256]{3,1,2,0:T(8,128)(2,1)} %get-tuple-element.36) | copy-start | bytes 1572868
  260.6 10.3 %collective-permute-start.9 = (bf16[1,32,1,64]{3,1,2,0:T(8,128)(2,1)S(1)}, bf16[1,32,1,64]{3,1,2,0:T(8,128)(2,1)S(1)}, u32[]{:S(2)}, u32[]{:S(2)}) collective-permute-start(bf16[1,32,1,64]{3,1,2,0:T(8,128)(2,1)S(1)} %get-tuple-element.69), channel_id=1, source_target_pairs={{16,0},{32,16},{48,32},{64,48},{80,64},{96,80},{112,96},{128,112},... | collective-permute-start | bytes 12296 | tf_op jit(solution)/shard_map/ppermute | solution.py:20
  262.1 8.8 %collective-permute-start.8 = (bf16[1,32,1,64]{3,1,2,0:T(8,128)(2,1)S(1)}, bf16[1,32,1,64]{3,1,2,0:T(8,128)(2,1)S(1)}, u32[]{:S(2)}, u32[]{:S(2)}) collective-permute-start(bf16[1,32,1,64]{3,1,2,0:T(8,128)(2,1)S(1)} %get-tuple-element.68), channel_id=1, source_target_pairs={{0,16},{16,32},{32,48},{48,64},{64,80},{80,96},{96,112},{112,128},... | collective-permute-start | bytes 12296 | tf_op jit(solution)/shard_map/ppermute | solution.py:17
  267.4 2.0 copy-start.3
  269.4 1.2 copy-start.10
  271.0 5.8 collective-permute-start.10
  275.2 9.8 %collective-permute-start.11 = (bf16[1,32,10,1]{3,1,2,0:T(8,128)(2,1)S(1)}, bf16[1,32,10,1]{3,1,2,0:T(8,128)(2,1)S(1)}, u32[]{:S(2)}, u32[]{:S(2)}) collective-permute-start(bf16[1,32,10,1]{3,1,2,0:T(8,128)(2,1)S(1)} %get-tuple-element.65), channel_id=1, source_target_pairs={{2,0},{4,2},{6,4},{8,6},{10,8},{12,10},{14,12},{3,1},{5,3},{7,5},{... | collective-permute-start | bytes 1928 | tf_op jit(solution)/shard_map/ppermute | solution.py:20
  292.1 4.8 copy-start.5
  296.9 6.8 %copy-start.14 = (bf16[1,32,32,256]{3,1,2,0:T(8,128)(2,1)S(1)}, bf16[1,32,32,256]{3,1,2,0:T(8,128)(2,1)}, u32[]{:S(2)}) copy-start(bf16[1,32,32,256]{3,1,2,0:T(8,128)(2,1)} %get-tuple-element.36) | copy-start | bytes 1572868
  298.4 5.7 collective-permute-start.13
  299.7 4.8 collective-permute-start.12
  304.8 9.4 %collective-permute-start.14 = (bf16[1,32,34,1]{3,1,2,0:T(8,128)(2,1)S(1)}, bf16[1,32,34,1]{3,1,2,0:T(8,128)(2,1)S(1)}, u32[]{:S(2)}, u32[]{:S(2)}) collective-permute-start(bf16[1,32,34,1]{3,1,2,0:T(8,128)(2,1)S(1)} %get-tuple-element.44), channel_id=1, source_target_pairs={{0,2},{2,4},{4,6},{6,8},{8,10},{10,12},{12,14},{1,3},{3,5},{5,7},{... | collective-permute-start | bytes 6536 | tf_op jit(solution)/shard_map/ppermute | solution.py:17
  310.6 9.0 %collective-permute-start.15 = (bf16[1,32,34,1]{3,1,2,0:T(8,128)(2,1)S(1)}, bf16[1,32,34,1]{3,1,2,0:T(8,128)(2,1)S(1)}, u32[]{:S(2)}, u32[]{:S(2)}) collective-permute-start(bf16[1,32,34,1]{3,1,2,0:T(8,128)(2,1)S(1)} %get-tuple-element.45), channel_id=1, source_target_pairs={{2,0},{4,2},{6,4},{8,6},{10,8},{12,10},{14,12},{3,1},{5,3},{7,5},{... | collective-permute-start | bytes 6536 | tf_op jit(solution)/shard_map/ppermute | solution.py:20
Sparse Core Ops, SparseCore 0:
  328.6 257.6 all-reduce.2
where the time goes:
time: 601 us; the launch traced here: 596 us
  waiting for transfers between devices  318 us (53%)
  local copies, waits for them, and re-layouts  149 us (25%)
  starting transfers between devices  74.9 us (12%)
  matrix products  25.9 us (4%)
  between operations  14.9 us (2%)
  other arithmetic  13.1 us (2%)
    psum x1, waiting for transfers between devices, shards(): lax.psum((first_grad, second_grad), ('rows', 'cols', 'dp'))  255 us
    gather x96, local copies, waits for them, and re-layouts  112 us
    ppermute x12, starting transfers between devices, padded(): lax.ppermute(lax.slice_in_dim(block, block.shape[dim] - width, None, axis...  58.8 us
    ppermute x12, waiting for transfers between devices, padded(): lax.ppermute(lax.slice_in_dim(block, 0, width, axis=dim), axis, backward)  38.3 us
    ppermute x12, waiting for transfers between devices, padded(): lax.ppermute(lax.slice_in_dim(block, block.shape[dim] - width, None, axis...  24.6 us
    ppermute x12, starting transfers between devices, padded(): lax.ppermute(lax.slice_in_dim(block, 0, width, axis=dim), axis, backward)  16 us
    broadcast_in_dim x6, local copies, waits for them, and re-layouts, upsample(): return jnp.repeat(jnp.repeat(values, POOL, axis=2), POOL, axis=3)  13 us
  transfers between devices with their start and end apart: 25, of which 13 were waited for; matrix products, arithmetic and copies ran while one was open for 5% of the time, Pallas kernels for 0%

commit v1 on v0

v1 whole, which is shorter than its diff:
```python
import functools
import math

import jax
import jax.numpy as jnp
from jax import lax
from jax.experimental import pallas as pl
from jax.experimental.pallas import tpu as pltpu
from jax.sharding import PartitionSpec as P

C = 32
R = 32
S = 256
M = 16
B = 8
K = (B + 2) * 3 * C
F32 = jnp.float32
BF16 = jnp.bfloat16
MESH = pl.DeviceIdType.MESH


def lanes(shape):
    return lax.broadcasted_iota(jnp.int32, shape, len(shape) - 1)


def roll(x, amount):
    size = x.shape[1]
    amount = amount % size
    return x if amount == 0 else pltpu.roll(x, amount, 1)


def banded(taps):
    wide = jnp.concatenate([taps, jnp.zeros((C, 640), F32)], axis=1)
    return jnp.concatenate([roll(wide, 96 * r) for r in range(B)], axis=0)[:, :K].astype(BF16)


def edge_flags():
    row, col = lax.axis_index("rows"), lax.axis_index("cols")
    nrows, ncols = lax.axis_size("rows"), lax.axis_size("cols")
    return (
        jnp.where(row > 0, 1.0, 0.0),
        jnp.where(row < nrows - 1, 1.0, 0.0),
        jnp.where(col > 0, 1.0, 0.0),
        jnp.where(col < ncols - 1, 1.0, 0.0),
    )


def pack_kernel(feat_ref, cot_ref, g_ref, ct_ref, left_ref, right_ref, fs, cs):
    for c in range(C):
        for t in range(2):
            fs[t, pl.ds(c, R, stride=C), :] = feat_ref[0, c, :, t * 128 : t * 128 + 128].astype(F32)
            cs[t, pl.ds(c, R, stride=C), :] = cot_ref[0, c, :, t * 128 : t * 128 + 128].astype(F32)
    for t in range(2):
        cols = slice(t * 128, t * 128 + 128)
        g_ref[C : C + R * C, cols] = fs[t].astype(BF16)
        g_ref[0:C, cols] = cs[t, 0:C, :].astype(BF16)
        g_ref[C + R * C :, cols] = cs[t, (R - 1) * C :, :].astype(BF16)
        ct_ref[:, cols] = cs[t].astype(BF16)
    lane = lanes((128, 128))
    for h in range(2):
        low = jnp.zeros((128, 128), F32)
        high = jnp.zeros((128, 128), F32)
        for g in range(4):
            base = (16 * h + 4 * g) * C
            here = (lane >= 32 * g) & (lane < 32 * g + 32)
            part = jnp.where(lane < 17, fs[0, base : base + 128, :], roll(cs[0, base : base + 128, :], 17))
            low = jnp.where(here, roll(part, 32 * g), low)
            part = jnp.where(
                lane < 17, roll(fs[1, base : base + 128, :], 17), roll(cs[1, base : base + 128, :], 18)
            )
            high = jnp.where(here, roll(part, 32 * g), high)
        left_ref[h * 128 : h * 128 + 128, :] = low.astype(BF16)
        right_ref[h * 128 : h * 128 + 128, :] = high.astype(BF16)


def vmem(n):
    return [pl.BlockSpec(memory_space=pltpu.VMEM)] * n


def pack(features, cotangent):
    return pl.pallas_call(
        pack_kernel,
        out_shape=(
            jax.ShapeDtypeStruct(((R + 2) * C, S), BF16),
            jax.ShapeDtypeStruct((R * C, S), BF16),
            jax.ShapeDtypeStruct((256, 128), BF16),
            jax.ShapeDtypeStruct((256, 128), BF16),
        ),
        in_specs=vmem(2),
        out_specs=tuple(vmem(4)),
        scratch_shapes=[pltpu.VMEM((2, R * C, 128), F32)] * 2,
        name="pack",
    )(features, cotangent)


def neighbours():
    row, col = lax.axis_index("rows"), lax.axis_index("cols")
    nrows, ncols = lax.axis_size("rows"), lax.axis_size("cols")
    rows = (lax.rem(row + nrows - 1, nrows), row, lax.rem(row + 1, nrows))
    cols = (lax.rem(col + ncols - 1, ncols), col, lax.rem(col + 1, ncols))
    return lambda dr, dc: {"rows": rows[dr + 1], "cols": cols[dc + 1]}


def exchange(plan, inputs, shapes, collective_id, name):
    count = len(inputs)

    def kernel(*refs):
        ins, outs = refs[:count], refs[count : count + len(shapes)]
        send, recv = refs[count + len(shapes) :]
        device = neighbours()
        barrier = pltpu.get_barrier_semaphore()
        for dr, dc, *_ in plan:
            pl.semaphore_signal(barrier, inc=1, device_id=device(dr, dc), device_id_type=MESH)
        pl.semaphore_wait(barrier, len(plan))
        copies = []
        for n, (dr, dc, source, rows, target) in enumerate(plan):
            src = ins[source] if rows is None else ins[source].at[rows[0] : rows[1], :]
            copy = pltpu.make_async_remote_copy(
                src_ref=src,
                dst_ref=outs[target],
                send_sem=send.at[n],
                recv_sem=recv.at[n],
                device_id=device(dr, dc),
                device_id_type=MESH,
            )
            copy.start()
            copies.append(copy)
        for copy in copies:
            copy.wait()

    return pl.pallas_call(
        kernel,
        out_shape=tuple(jax.ShapeDtypeStruct(s, BF16) for s in shapes),
        in_specs=vmem(count),
        out_specs=tuple(vmem(len(shapes))),
        scratch_shapes=[pltpu.SemaphoreType.DMA((len(plan),)), pltpu.SemaphoreType.DMA((len(plan),))],
        compiler_params=pltpu.CompilerParams(collective_id=collective_id, has_side_effects=True),
        name=name,
    )(*inputs)


def exchange_inputs(g, left, right):
    plan = (
        (-1, 0, 0, (0, 18 * C), 1),
        (1, 0, 0, (16 * C, 34 * C), 0),
        (0, -1, 1, None, 3),
        (0, 1, 2, None, 2),
        (-1, -1, 1, (0, 160), 7),
        (1, -1, 1, (96, 256), 5),
        (-1, 1, 2, (0, 160), 6),
        (1, 1, 2, (96, 256), 4),
    )
    shapes = [(18 * C, S)] * 2 + [(256, 128)] * 2 + [(160, 128)] * 4
    return exchange(plan, (g, left, right), shapes, 0, "exchange_inputs")


def exchange_edges(up, down, left, right):
    plan = (
        (-1, 0, 0, None, 1),
        (1, 0, 1, None, 0),
        (0, -1, 2, None, 3),
        (0, 1, 3, None, 2),
        (-1, -1, 2, None, 7),
        (1, -1, 2, None, 5),
        (-1, 1, 3, None, 6),
        (1, 1, 3, None, 4),
    )
    shapes = [(160, 128)] * 2 + [(C, 128)] * 6
    return exchange(plan, (up, down, left, right), shapes, 1, "exchange_edges")


def with_edges(x, left, right):
    lane = lanes((x.shape[0], 128))
    back = pltpu.roll(x, 1, 1)
    ahead = pltpu.roll(x, S - 1, 1)
    back = jnp.concatenate([jnp.where(lane == 0, left, back[:, 0:128]), back[:, 128:256]], axis=1)
    ahead = jnp.concatenate([ahead[:, 0:128], jnp.where(lane == 127, right, ahead[:, 128:256])], axis=1)
    return back, x, ahead


def store_three(ref, first_row, versions):
    for b in range(3):
        value = versions[b].astype(BF16)
        for n in range(value.shape[0] // C):
            at = (first_row + n) * 96 + b * C
            ref[at : at + C, :] = value[n * C : n * C + C, :]


def first_kernel_body(
    shift_ref, g_ref, ct_ref, up_ref, down_ref, left_ref, right_ref, ul_ref, ur_ref, dl_ref, dr_ref, tap_ref,
    act_ref, slope_ref, bg_ref, pool_ref, coarse_ref, x3_ref, mu_ref, md_ref, el_ref, er_ref,
    fe, xf, c3,
):
    has_up, has_down, has_left, has_right = edge_flags()

    for t in range(2):
        cols = slice(t * 128, t * 128 + 128)
        fe[t + 1, 0 : 17 * C, :] = up_ref[0 : 17 * C, cols].astype(F32) * has_up
        fe[t + 1, 17 * C : 49 * C, :] = g_ref[C : 33 * C, cols].astype(F32)
        fe[t + 1, 49 * C :, :] = down_ref[C : 18 * C, cols].astype(F32) * has_down
    for side, (u, m, d), offset, flag in (
        (0, (ul_ref, left_ref, dl_ref), 111, has_left),
        (3, (ur_ref, right_ref, dr_ref), 0, has_right),
    ):
        above, below = flag * has_up, flag * has_down
        fe[side, 0:C, :] = roll(u[0:C, :].astype(F32), offset - 96) * above
        fe[side, 65 * C :, :] = roll(d[128:160, :].astype(F32), offset) * below
        for g in range(4):
            turn = offset - 32 * g
            at = (1 + 4 * g) * C
            fe[side, at : at + 128, :] = roll(u[32:160, :].astype(F32), turn) * above
            at = (49 + 4 * g) * C
            fe[side, at : at + 128, :] = roll(d[0:128, :].astype(F32), turn) * below
            for h in range(2):
                at = (17 + 16 * h + 4 * g) * C
                fe[side, at : at + 128, :] = roll(m[h * 128 : h * 128 + 128, :].astype(F32), turn) * flag

    for c in range(C):
        row_shift, col_shift = shift_ref[0, c, 0], shift_ref[0, c, 1]
        x = jnp.concatenate(
            [fe[t, pl.ds((M + row_shift) * C + c, R + 2, stride=C), :] for t in range(4)], axis=1
        )
        for b in range(3):
            y = pltpu.roll(x, 385 - b - col_shift, 1)
            for t in range(2):
                xf[t, pl.ds(b * C + c, R + 2, stride=96), :] = y[:, t * 128 : t * 128 + 128]
    lane = lanes((C, S))
    first_lane = jnp.where(lane == 0, has_left, 1.0)
    last_lane = jnp.where(lane == S - 1, has_right, 1.0)
    for row in range(R + 2):
        scale = has_up if row == 0 else has_down if row == R + 1 else None
        for b in range(3):
            at = row * 96 + b * C
            value = jnp.concatenate([xf[0, at : at + C, :], xf[1, at : at + C, :]], axis=1)
            if b != 1:
                value = value * (first_lane if b == 0 else last_lane)
            if scale is not None:
                value = value * scale
            x3_ref[at : at + C, :] = value.astype(BF16)

    for h in range(2):
        for g in range(4):
            base = 16 * h + 4 * g
            left = roll(left_ref[h * 128 : h * 128 + 128, :].astype(F32), -(32 * g + 17)) * has_left
            right = roll(right_ref[h * 128 : h * 128 + 128, :].astype(F32), 127 - (32 * g + 17)) * has_right
            x = ct_ref[base * C : base * C + 128, :].astype(F32)
            store_three(c3, base + 1, with_edges(x, left, right))
    left = roll(ul_ref[128:160, :].astype(F32), -(96 + 17)) * (has_left * has_up)
    right = roll(ur_ref[128:160, :].astype(F32), 127 - (96 + 17)) * (has_right * has_up)
    store_three(c3, 0, with_edges(up_ref[17 * C :, :].astype(F32) * has_up, left, right))
    left = roll(dl_ref[0:32, :].astype(F32), -17) * (has_left * has_down)
    right = roll(dr_ref[0:32, :].astype(F32), 127 - 17) * (has_right * has_down)
    store_three(c3, R + 1, with_edges(down_ref[0:C, :].astype(F32) * has_down, left, right))

    weights = banded(tap_ref[0])
    back_weights = banded(tap_ref[2])
    cell = 32 + lax.shift_right_logical(lax.broadcasted_iota(jnp.int32, (S, 128), 0), 2)
    gather = jnp.where(cell == lanes((S, 128)), 1.0, 0.0).astype(BF16)
    for k in range(R // B):
        rows = slice(k * B * C, (k + 1) * B * C)
        depth = slice(k * B * 96, k * B * 96 + K)
        pre = jnp.dot(weights, x3_ref[depth, :], preferred_element_type=F32)
        sigma = 1.0 / (1.0 + jnp.exp(-pre))
        act = (pre * sigma).astype(BF16)
        act_ref[rows, :] = act
        slope_ref[rows, :] = sigma * (1.0 + pre * (1.0 - sigma))
        bg = jnp.dot(back_weights, c3[depth, :], preferred_element_type=F32).astype(BF16)
        bg_ref[rows, :] = bg
        for value, ref, factor in ((act, pool_ref, 1.0 / 16.0), (bg, coarse_ref, 1.0)):
            sums = jnp.dot(value, gather, preferred_element_type=F32)
            for j in range(2):
                four = sums[j * 128 : j * 128 + 128]
                four = (four[0:32] + four[32:64]) + (four[64:96] + four[96:128])
                at = (2 * k + j) * C
                ref[at : at + C, :] = (four * factor).astype(BF16)

    mu_ref[0:32, :] = act_ref[0:32, 0:128]
    mu_ref[32:64, :] = act_ref[0:32, 128:256]
    mu_ref[64:128, :] = pool_ref[0:64, :]
    mu_ref[128:160, :] = coarse_ref[0:32, :]
    md_ref[0:32, :] = act_ref[31 * C :, 0:128]
    md_ref[32:64, :] = act_ref[31 * C :, 128:256]
    md_ref[64:128, :] = pool_ref[192:256, :]
    md_ref[128:160, :] = coarse_ref[224:256, :]
    lane = lanes((C, 128))
    low = jnp.zeros((C, 128), F32)
    high = jnp.zeros((C, 128), F32)
    for j in range(8):
        for v in range(4):
            at = (4 * j + v) * C
            t = 8 * j + v
            low = jnp.where(lane == t, roll(act_ref[at : at + C, 0:128].astype(F32), t), low)
            high = jnp.where(lane == t, roll(act_ref[at : at + C, 128:256].astype(F32), t - 127), high)
        t = 8 * j + 4
        two = (lane == t) | (lane == t + 1)
        value = pool_ref[j * C : j * C + C, :].astype(F32)
        low = jnp.where(two, roll(value, t - 32), low)
        high = jnp.where(two, roll(value, t - 94), high)
        t = 8 * j + 6
        value = coarse_ref[j * C : j * C + C, :].astype(F32)
        low = jnp.where(lane == t, roll(value, t - 32), low)
        high = jnp.where(lane == t, roll(value, t - 95), high)
    el_ref[...] = low.astype(BF16)
    er_ref[...] = high.astype(BF16)


def first_half(shifts, g, ct, halos, taps):
    shapes = (
        ((R * C, S), BF16),
        ((R * C, S), F32),
        ((R * C, S), BF16),
        ((256, 128), BF16),
        ((256, 128), BF16),
        (((R + 2) * 96, S), BF16),
        ((160, 128), BF16),
        ((160, 128), BF16),
        ((C, 128), BF16),
        ((C, 128), BF16),
    )
    return pl.pallas_call(
        first_kernel_body,
        out_shape=tuple(jax.ShapeDtypeStruct(s, d) for s, d in shapes),
        in_specs=[pl.BlockSpec(memory_space=pltpu.SMEM)] + vmem(11),
        out_specs=tuple(vmem(10)),
        scratch_shapes=[
            pltpu.VMEM((4, 66 * C, 128), F32),
            pltpu.VMEM((2, (R + 2) * 96, 128), F32),
            pltpu.VMEM(((R + 2) * 96, S), BF16),
        ],
        name="first_half",
    )(shifts, g, ct, *halos, taps)


def halves(x):
    high = x.astype(BF16)
    low = (x - high.astype(F32)).astype(BF16)
    return jnp.concatenate([high, low], axis=1)


def spread(b):
    cell = lax.rem(lax.broadcasted_iota(jnp.int32, (256, S), 0), 128)
    want = 31 + lax.shift_right_logical(lanes((256, S)) + (b - 1 + 4), 2)
    return jnp.where(cell == want, 1.0, 0.0).astype(BF16)


def collected(total, factor):
    groups = []
    for m in range(4):
        groups.append(
            total[m * 96 : m * 96 + 288, 0:128] + total[(m + 4) * 96 : (m + 4) * 96 + 288, 128:256]
        )
    lane = lanes((72, 128))
    result = jnp.zeros((72, 128), F32)
    for q in range(4):
        part = slice(72 * q, 72 * q + 72)
        value = sum(roll(groups[m][part], 32 * (q - m)) for m in range(4))
        result = jnp.where((lane >= 32 * q) & (lane < 32 * q + 32), value, result)
    return result * factor


def contract(a, b):
    return lax.dot_general(a, b, (((1,), (1,)), ((), ())), preferred_element_type=F32)


def second_kernel_body(
    factor,
    act_ref, slope_ref, bg_ref, pool_ref, coarse_ref, x3_ref, ct_ref,
    mu_ref, md_ref, el_ref, er_ref, ul_ref, ur_ref, dl_ref, dr_ref, tap_ref,
    pred_ref, grad_ref,
    p3, b3, pg, pf, up0, up1, up2,
):
    has_up, has_down, has_left, has_right = edge_flags()
    lane = lanes((C, 128))
    left_tiles = [ul_ref] * 2 + [el_ref] * 8 + [dl_ref] * 2
    right_tiles = [ur_ref] * 2 + [er_ref] * 8 + [dr_ref] * 2

    def coarse_rows(width, centre):
        first_row = -width
        for row in range(-width, 8 + width):
            j = row % 8
            above = has_up if row < 0 else has_down if row >= 8 else 1.0
            t = 8 * j + (4 if width == 2 else 6)
            span = 2 if width == 2 else 1
            x = centre(row).astype(F32)
            left = roll(left_tiles[row + 2][...].astype(F32), 32 - span - t)
            right = roll(right_tiles[row + 2][...].astype(F32), 96 - t)
            x = jnp.where((lane >= 32 - span) & (lane < 32), left * has_left, x)
            x = jnp.where((lane >= 96) & (lane < 96 + span), right * has_right, x)
            if row < 0 or row >= 8:
                x = x * above
            for b in range(3):
                at = (row - first_row) * 96 + b * C
                p3[at : at + C, :] = roll(x, 1 - b).astype(BF16)

    def pooled_row(row):
        if row < 0:
            return mu_ref[64 + (row + 2) * C : 64 + (row + 3) * C, :]
        if row >= 8:
            return md_ref[64 + (row - 8) * C : 64 + (row - 7) * C, :]
        return pool_ref[row * C : row * C + C, :]

    def coarse_row(row):
        if row < 0:
            return mu_ref[128:160, :]
        if row >= 8:
            return md_ref[128:160, :]
        return coarse_ref[row * C : row * C + C, :]

    coarse_rows(2, pooled_row)
    weights = banded(tap_ref[3])
    bottle = jnp.concatenate(
        [
            jnp.dot(weights, p3[0:K, :], preferred_element_type=F32),
            jnp.dot(weights, p3[192 : 192 + K, :], preferred_element_type=F32)[6 * C :],
        ],
        axis=0,
    )
    parts = halves(bottle)
    for b, ref in enumerate((up0, up1, up2)):
        ref[...] = jnp.dot(parts, spread(b), preferred_element_type=F32)

    for row in range(-1, R + 1):
        if row < 0:
            x = jnp.concatenate([mu_ref[0:32, :], mu_ref[32:64, :]], axis=1).astype(F32)
            low, high, t = ul_ref, ur_ref, 59
        elif row == R:
            x = jnp.concatenate([md_ref[0:32, :], md_ref[32:64, :]], axis=1).astype(F32)
            low, high, t = dl_ref, dr_ref, 0
        else:
            x = act_ref[row * C : row * C + C, :].astype(F32)
            low, high, t = el_ref, er_ref, 8 * (row // 4) + row % 4
        at = ((row + 4) // 4) * C
        ups = [ref[at : at + C, :] for ref in (up0, up1, up2)]
        back, mid, ahead = with_edges(x, roll(low[...].astype(F32), -t), roll(high[...].astype(F32), 127 - t))
        wide = lanes((C, S))
        back = (back + ups[0]) * jnp.where(wide == 0, has_left, 1.0)
        mid = mid + ups[1]
        ahead = (ahead + ups[2]) * jnp.where(wide == S - 1, has_right, 1.0)
        if row < 0 or row == R:
            keep = has_up if row < 0 else has_down
            back, mid, ahead = back * keep, mid * keep, ahead * keep
        store_three(b3, row + 1, (back, mid, ahead))

    coarse_rows(1, coarse_row)
    weights = banded(tap_ref[4])
    grad = jnp.dot(weights, p3[0:K, :], preferred_element_type=F32)
    up1[0:256, :] = jnp.dot(halves(grad), spread(1), preferred_element_type=F32) * (1.0 / 16.0)
    for row in range(R):
        at = slice(row * C, row * C + C)
        cell = (row // 4) * C
        value = (bg_ref[at, :].astype(F32) + up1[cell : cell + C, :]) * slope_ref[at, :]
        pg[at, :] = value.astype(BF16)

    weights = banded(tap_ref[1])
    first = second = None
    for k in range(R // B):
        rows = slice(k * B * C, (k + 1) * B * C)
        depth = slice(k * B * 96, k * B * 96 + K)
        value = jnp.dot(weights, b3[depth, :], preferred_element_type=F32)
        pf[0, rows, :] = value[:, 0:128]
        pf[1, rows, :] = value[:, 128:256]
        one = contract(b3[depth, :], ct_ref[rows, :])
        two = contract(x3_ref[depth, :], pg[rows, :])
        second = one if second is None else second + one
        first = two if first is None else first + two
    for o in range(C):
        for t in range(2):
            pred_ref[0, o, :, t * 128 : t * 128 + 128] = pf[t, pl.ds(o, R, stride=C), :].astype(BF16)
    both = jnp.concatenate([collected(first, factor), collected(second, factor)], axis=0)
    pieces, height = grad_ref.shape[:2]
    for n in range(pieces):
        grad_ref[n] = both[n * height : (n + 1) * height, :]


def second_half(factor, pieces, first, ct, edges, taps):
    act, slope, bg, pool, coarse, x3 = first
    return pl.pallas_call(
        functools.partial(second_kernel_body, factor),
        out_shape=(
            jax.ShapeDtypeStruct((1, C, R, S), BF16),
            jax.ShapeDtypeStruct((pieces, 144 // pieces, 128), F32),
        ),
        in_specs=vmem(16),
        out_specs=tuple(vmem(2)),
        scratch_shapes=[
            pltpu.VMEM((12 * 96, 128), BF16),
            pltpu.VMEM(((R + 2) * 96, S), BF16),
            pltpu.VMEM((R * C, S), BF16),
            pltpu.VMEM((2, R * C, 128), F32),
            pltpu.VMEM((10 * C, S), F32),
            pltpu.VMEM((10 * C, S), F32),
            pltpu.VMEM((10 * C, S), F32),
        ],
        name="second_half",
    )(act, slope, bg, pool, coarse, x3, ct, *edges, taps)


def reduce_kernel(grad_ref, out_ref, held, mine, column, send_a, recv_a, send_b, recv_b, send_c, recv_c):
    row, col, img = lax.axis_index("rows"), lax.axis_index("cols"), lax.axis_index("dp")
    nrows, ncols, ndp = lax.axis_size("rows"), lax.axis_size("cols"), lax.axis_size("dp")
    pieces = ncols * ndp
    me = col * ndp + img

    def peer(d):
        other = lax.rem(me + d, pieces)
        return other, {"cols": other // ndp, "dp": lax.rem(other, ndp)}

    def in_column(d):
        return {"rows": lax.rem(row + d, nrows)}

    barrier = pltpu.get_barrier_semaphore()
    for d in range(1, pieces):
        pl.semaphore_signal(barrier, inc=1, device_id=peer(d)[1], device_id_type=MESH)
    for d in range(1, nrows):
        pl.semaphore_signal(barrier, inc=1, device_id=in_column(d), device_id_type=MESH)
    pl.semaphore_wait(barrier, pieces + nrows - 2)

    copies = []
    for d in range(1, pieces):
        other, device = peer(d)
        copies.append(
            pltpu.make_async_remote_copy(
                src_ref=grad_ref.at[other],
                dst_ref=held.at[d],
                send_sem=send_a.at[d],
                recv_sem=recv_a.at[d],
                device_id=device,
                device_id_type=MESH,
            )
        )
        copies[-1].start()
    total = grad_ref[me]
    for d in range(1, pieces):
        copies[d - 1].wait_recv()
        total = total + held[d]
    mine[...] = total
    column[row] = total
    for d in range(1, nrows):
        copies.append(
            pltpu.make_async_remote_copy(
                src_ref=mine,
                dst_ref=column.at[row],
                send_sem=send_b.at[d],
                recv_sem=recv_b.at[d],
                device_id=in_column(d),
                device_id_type=MESH,
            )
        )
        copies[-1].start()
    for d in range(1, nrows):
        copies[pieces - 2 + d].wait_recv()
    total = column[0]
    for n in range(1, nrows):
        total = total + column[n]
    out_ref[me] = total
    for d in range(1, pieces):
        copies.append(
            pltpu.make_async_remote_copy(
                src_ref=out_ref.at[me],
                dst_ref=out_ref.at[me],
                send_sem=send_c.at[d],
                recv_sem=recv_c.at[d],
                device_id=peer(d)[1],
                device_id_type=MESH,
            )
        )
        copies[-1].start()
    for d in range(1, pieces):
        copies[pieces + nrows - 3 + d].wait_recv()
    for copy in copies:
        copy.wait_send()


def reduce_all(grads):
    pieces, height = grads.shape[:2]
    nrows = lax.axis_size("rows")
    piece = pltpu.VMEM((height, 128), F32)
    return pl.pallas_call(
        reduce_kernel,
        out_shape=jax.ShapeDtypeStruct(grads.shape, F32),
        in_specs=vmem(1),
        out_specs=vmem(1)[0],
        scratch_shapes=[
            pltpu.VMEM((pieces, height, 128), F32),
            piece,
            pltpu.VMEM((nrows, height, 128), F32),
        ]
        + [pltpu.SemaphoreType.DMA((n,)) for n in (pieces, pieces, nrows, nrows, pieces, pieces)],
        compiler_params=pltpu.CompilerParams(collective_id=2, has_side_effects=True),
        name="reduce_all",
    )(grads)


def tap_rows(kernel, transpose):
    if transpose:
        kernel = kernel[::-1]
    taps = kernel.reshape(3, 3, C, C).transpose((3, 0, 1, 2) if transpose else (2, 0, 1, 3))
    return jnp.pad(taps.reshape(C, 9 * C), ((0, 0), (0, 384 - 9 * C)))


def shards(features, shifts, first_kernel, bottle_kernel, second_kernel, cotangent):
    nrows, ncols, ndp = lax.axis_size("rows"), lax.axis_size("cols"), lax.axis_size("dp")
    assert features.shape == (1, C, R, S)
    taps = jnp.stack(
        [
            tap_rows(first_kernel, False),
            tap_rows(second_kernel, False),
            tap_rows(second_kernel, True),
            tap_rows(bottle_kernel, False),
            tap_rows(bottle_kernel, True),
        ]
    ).astype(F32)
    g, ct, left, right = pack(features, cotangent)
    halos = exchange_inputs(g, left, right)
    *first, mu, md, el, er = first_half(shifts, g, ct, halos, taps)
    edges = exchange_edges(mu, md, el, er)
    factor = 1.0 / math.sqrt(ndp * nrows * R * ncols * S)
    prediction, grads = second_half(factor, ncols * ndp, first, ct, edges, taps)
    grads = reduce_all(grads).reshape(2, 72, 4, C).transpose(0, 2, 1, 3)
    grads = grads.reshape(2, 9, C, C).transpose(0, 1, 3, 2)
    return prediction, grads[0], grads[1]


def solution(mesh):
    placed = (
        P("dp", None, "rows", "cols"),
        P("dp", None, None),
        P(),
        P(),
        P(),
        P("dp", None, "rows", "cols"),
    )
    return jax.shard_map(
        shards,
        mesh=mesh,
        in_specs=placed,
        out_specs=(P("dp", None, "rows", "cols"), P(), P()),
        check_vma=False,
    )
```

time: 601 us -> 90.6 us (0.15)
  waiting for transfers between devices: 318 us -> 0 us
  local copies, waits for them, and re-layouts: 149 us -> 8.65 us
  Pallas kernels: 0 us -> 80 us
  starting transfers between devices: 74.9 us -> 0 us
  matrix products: 25.9 us -> 0 us
  between operations: 14.9 us -> 0.74 us
  other arithmetic: 13.1 us -> 0.74 us
    psum x1 -> x0, waiting for transfers between devices: 255 us -> none  [shards(): lax.psum((first_grad, second_grad), ('rows', 'cols', 'dp'))]
    gather x96 -> x0, local copies, waits for them, and re-layouts: 112 us -> none
    pallas_call x0 -> x6, Pallas kernels: none -> 80 us  [the longest x2 35 us: exchange(): pl.pallas_call(kernel, out_shape=tuple((jax.ShapeDtypeStruct(s, BF16) for...]
    ppermute x24 -> x0, starting transfers between devices: 74.8 us -> none  [the longest x12 58.8 us: padded(): lax.ppermute(lax.slice_in_dim(block, block.shape[dim] - width, None, axis...]
    ppermute x24 -> x0, waiting for transfers between devices: 62.9 us -> none  [the longest x12 38.3 us: padded(): lax.ppermute(lax.slice_in_dim(block, 0, width, axis=dim), axis, backward)]
    dot_general x63 -> x0, matrix products: 25.9 us -> none  [the longest x27 10.8 us: convolve_ext(): jnp.einsum('oi,bihw->bohw', kernel[tap_index], window, preferred_element_...]
    broadcast_in_dim x6 -> x0, local copies, waits for them, and re-layouts: 13 us -> none  [upsample(): return jnp.repeat(jnp.repeat(values, POOL, axis=2), POOL, axis=3)]
    reduce_sum x2 -> x0, other arithmetic: 7.2 us -> none  [pool_sum(): values.reshape(shape[0], shape[1], shape[2] // POOL, POOL, shape[3] // PO...]
  transfers between devices with their start and end apart: 25 -> 0, of which waited for: 13 -> 0; matrix products, arithmetic and copies ran while one was open for 5% -> 0% of each run, Pallas kernels for 0% -> 0%
where the time goes in v1:
time: 90.6 us; the launch traced here: 90.2 us
  Pallas kernels  80 us (88%)
  local copies, waits for them, and re-layouts  8.65 us (10%)
    pallas_call x2, Pallas kernels, exchange(): pl.pallas_call(kernel, out_shape=tuple((jax.ShapeDtypeStruct(s, BF16) for...  35 us
    pallas_call x1, Pallas kernels, reduce_all(): pl.pallas_call(reduce_kernel, out_shape=jax.ShapeDtypeStruct(grads.shape,...  23.6 us
    pallas_call x1, Pallas kernels, first_half(): pl.pallas_call(first_kernel_body, out_shape=tuple((jax.ShapeDtypeStruct(s...  10.8 us
    pallas_call x1, Pallas kernels, second_half(): pl.pallas_call(functools.partial(second_kernel_body, factor), out_shape=(...  6.68 us
    pallas_call x1, Pallas kernels, pack(): pl.pallas_call(pack_kernel, out_shape=(jax.ShapeDtypeStruct(((R + 2) * C,...  3.97 us
    unnamed x9, local copies, waits for them, and re-layouts  2.99 us
    reshape x5, local copies, waits for them, and re-layouts, tap_rows(): kernel.reshape(3, 3, C, C)  2.18 us

profile of v1, /device:TPU:1, one launch (start us, length us, event | category | flops | bytes accessed | tf_op | source)
XLA Modules:
  0.0 90.2 jit_solution(9347406607749528536)
XLA Ops:
  0.6 0.0 copy-start
  0.6 1.4 %copy.20.shift_ref = s32[1,32,2]{2,1,0:T(8,128)} copy(s32[1,32,2]{1,2,0:T(2,128)} %param.7) | data formatting | bytes 512 | tf_op args[1]
  2.0 0.9 rev.7
  2.9 0.1 copy.19
  3.1 0.1 reshape.51
  3.2 0.9 rev.6
  4.1 0.1 copy.17
  4.2 0.1 reshape.47
  4.3 0.9 %copy.29 = bf16[3,3,32,32]{3,1,0,2:T(4,128)(2,1)S(1)} copy(bf16[3,3,32,32]{3,2,1,0:T(8,128)(2,1)} %bitcast.45) | data formatting | bytes 36864 | tf_op jit(solution)/shard_map/reshape | solution.py:597
  5.2 0.1 reshape.43
  5.4 0.9 %copy.28 = bf16[3,3,32,32]{3,1,0,2:T(4,128)(2,1)S(1)} copy(bf16[3,3,32,32]{3,2,1,0:T(8,128)(2,1)} %bitcast.41) | data formatting | bytes 36864 | tf_op jit(solution)/shard_map/reshape | solution.py:597
  6.3 0.1 reshape.45
  6.5 0.0 copy-done
  6.5 0.1 copy.27
  6.5 0.1 reshape.49
  6.7 0.7 convert_element_type.9.tap_ref
  7.4 4.0 %pack.1 = (bf16[1088,256]{1,0:T(8,128)(2,1)}, bf16[1024,256]{1,0:T(8,128)(2,1)}, bf16[256,128]{1,0:T(8,128)(2,1)}, bf16[256,128]{1,0:T(8,128)(2,1)}) custom-call(bf16[1,32,32,256]{3,2,1,0:T(8,128)(2,1)} %feat_ref.1, bf16[1,32,32,256]{3,2,1,0:T(8,128)(2,1)} %cot_ref.1), custom_call_target="tpu_custom_call" | custom-call | tf_op jit(solution)/shard_map/pack/pallas_call | solution.py:81
  11.4 24.7 %exchange_inputs.1 = (bf16[576,256]{1,0:T(8,128)(2,1)}, bf16[576,256]{1,0:T(8,128)(2,1)}, bf16[256,128]{1,0:T(8,128)(2,1)}, bf16[256,128]{1,0:T(8,128)(2,1)}, bf...) custom-call(bf16[1088,256]{1,0:T(8,128)(2,1)} %get-tuple-element.35.refs, ...), custom_call_target="tpu_custom_call" | custom-call | tf_op jit(solution)/shard_map/exchange_inputs/pallas_call | solution.py:131
  36.1 10.8 %first_half.1 = (bf16[1024,256]{1,0:T(8,128)(2,1)}, f32[1024,256]{1,0:T(8,128)}, bf16[1024,256]{1,0:T(8,128)(2,1)}, bf16[256,128]{1,0:T(8,128)(2,1)}, bf16[256,1...) custom-call(s32[1,32,2]{2,1,0:T(8,128)} %copy.20.shift_ref, ...), custom_call_target="tpu_custom_call" | custom-call | tf_op jit(solution)/shard_map/first_half/pallas_call | solution.py:320
  46.8 10.3 %exchange_edges.1 = (bf16[160,128]{1,0:T(8,128)(2,1)}, bf16[160,128]{1,0:T(8,128)(2,1)}, bf16[32,128]{1,0:T(8,128)(2,1)}, bf16[32,128]{1,0:T(8,128)(2,1)}, bf16[...) custom-call(bf16[160,128]{1,0:T(8,128)(2,1)} %get-tuple-element.53.refs_0_, ...), custom_call_target="tpu_custom_call" | custom-call | tf_op jit(solution)/shard_map/exchange_edges/pallas_call | solution.py:131
  57.2 6.7 %second_half.1 = (bf16[1,32,32,256]{3,2,1,0:T(8,128)(2,1)}, f32[16,9,128]{2,1,0:T(8,128)}) custom-call(bf16[1024,256]{1,0:T(8,128)(2,1)} %get-tuple-element.47.act_ref, f32[1024,256]{1,0:T(8,128)} %get-tuple-element.48.slope_ref, bf16[1024,256]{1,0:T(8,128)(2,1)} %get-tuple-element.49.bg_ref, bf16[256,128]{1,0:T(8,128)(2,1)} %get-tuple-element.50.pool_ref, ...), custom_call_target="tpu_custom_call" | custom-call | tf_op jit(solution)/shard_map/second_half/pallas_call | solution.py:477
  63.8 23.6 %reduce_all.1 = f32[16,9,128]{2,1,0:T(8,128)} custom-call(f32[16,9,128]{2,1,0:T(8,128)} %get-tuple-element.66.grad_ref), custom_call_target="tpu_custom_call" | custom-call | tf_op jit(solution)/shard_map/reduce_all/pallas_call | solution.py:578
  87.5 1.1 %reshape.52 = f32[2,72,4,32]{3,2,1,0:T(4,128)S(1)} reshape(f32[16,9,128]{2,1,0:T(8,128)} %reduce_all.1) | data formatting | bytes 147456 | tf_op jit(solution)/shard_map/reshape | solution.py:619
  88.6 0.8 copy.23
  89.4 0.8 copy.22
  (7 shorter events, 0.1 us)
Async XLA Ops:
  0.6 5.8 %copy-start = (bf16[9,32,32]{2,1,0:T(8,128)(2,1)S(1)}, bf16[9,32,32]{2,1,0:T(8,128)(2,1)}, u32[]{:S(2)}) copy-start(bf16[9,32,32]{2,1,0:T(8,128)(2,1)} %param.9) | copy-start | bytes 55300

commit v2 on v0

v2 whole, which is shorter than its diff:
```python
import functools
import math

import jax
import jax.numpy as jnp
from jax import lax
from jax.experimental import pallas as pl
from jax.experimental.pallas import tpu as pltpu
from jax.sharding import PartitionSpec as P

C = 32
R = 32
S = 256
M = 16
B = 8
K = (B + 2) * 3 * C
F32 = jnp.float32
BF16 = jnp.bfloat16
MESH = pl.DeviceIdType.MESH


def lanes(shape):
    return lax.broadcasted_iota(jnp.int32, shape, len(shape) - 1)


def roll(x, amount):
    size = x.shape[1]
    amount = amount % size
    return x if amount == 0 else pltpu.roll(x, amount, 1)


def banded(taps):
    wide = jnp.concatenate([taps, jnp.zeros((C, 1024 - 9 * C), F32)], axis=1)
    return jnp.concatenate([roll(wide, 96 * r) for r in range(B)], axis=0)[:, :K].astype(BF16)


def forward_taps(ref):
    return jnp.concatenate([ref[t].astype(F32) for t in range(9)], axis=1)


def backward_taps(ref):
    return jnp.concatenate([ref[8 - t].astype(F32) for t in range(9)], axis=0).T


def edge_flags():
    row, col = lax.axis_index("rows"), lax.axis_index("cols")
    nrows, ncols = lax.axis_size("rows"), lax.axis_size("cols")
    return (
        jnp.where(row > 0, 1.0, 0.0),
        jnp.where(row < nrows - 1, 1.0, 0.0),
        jnp.where(col > 0, 1.0, 0.0),
        jnp.where(col < ncols - 1, 1.0, 0.0),
    )


def neighbours():
    row, col = lax.axis_index("rows"), lax.axis_index("cols")
    nrows, ncols = lax.axis_size("rows"), lax.axis_size("cols")
    rows = (lax.rem(row + nrows - 1, nrows), row, lax.rem(row + 1, nrows))
    cols = (lax.rem(col + ncols - 1, ncols), col, lax.rem(col + 1, ncols))
    return lambda dr, dc: {"rows": rows[dr + 1], "cols": cols[dc + 1]}


def with_edges(x, left, right):
    lane = lanes((x.shape[0], 128))
    back = pltpu.roll(x, 1, 1)
    ahead = pltpu.roll(x, S - 1, 1)
    back = jnp.concatenate([jnp.where(lane == 0, left, back[:, 0:128]), back[:, 128:256]], axis=1)
    ahead = jnp.concatenate([ahead[:, 0:128], jnp.where(lane == 127, right, ahead[:, 128:256])], axis=1)
    return back, x, ahead


def store_three(ref, first_row, versions):
    for b in range(3):
        value = versions[b].astype(BF16)
        for n in range(value.shape[0] // C):
            at = (first_row + n) * 96 + b * C
            ref[at : at + C, :] = value[n * C : n * C + C, :]


def halves(x):
    high = x.astype(BF16)
    low = (x - high.astype(F32)).astype(BF16)
    return jnp.concatenate([high, low], axis=1)


def spread(b):
    cell = lax.rem(lax.broadcasted_iota(jnp.int32, (256, S), 0), 128)
    want = 31 + lax.shift_right_logical(lanes((256, S)) + (b - 1 + 4), 2)
    return jnp.where(cell == want, 1.0, 0.0).astype(BF16)


def contract(a, b):
    return lax.dot_general(a, b, (((1,), (1,)), ((), ())), preferred_element_type=F32)


def collected(total, factor):
    result = None
    for r in range(B):
        block = total[r * C : r * C + C, :]
        block = roll(jnp.concatenate([block, jnp.zeros((C, 1024 - K), F32)], axis=1), -96 * r)[:, 0:384]
        result = block if result is None else result + block
    return result * factor


def ring_plan(up, down, left, right, left_up=None, left_down=None, right_up=None, right_down=None):
    return (
        (1, 0, down, 0),
        (-1, 0, up, 1),
        (0, 1, right, 2),
        (0, -1, left, 3),
        (1, 1, right if right_down is None else right_down, 4),
        (1, -1, left if left_down is None else left_down, 5),
        (-1, 1, right if right_up is None else right_up, 6),
        (-1, -1, left if left_up is None else left_up, 7),
    )


def half(x, t):
    return x[:, t * 128 : t * 128 + 128]


def both_halves(ref, rows):
    return jnp.concatenate([ref[0, rows, :], ref[1, rows, :]], axis=1)


def main_kernel(
    factor,
    feat_ref, cot_ref, shift_hbm, k1_ref, kb_ref, k2_ref,
    pred_ref, grad_ref,
    shift_ref, fs, cs, ft, ct, sl, sr, cl, cr, fe, xf, x3, c3, w1, w2, w2t, wb, wbt,
    act, slope, bg, pool, coarse, mu, md, el, er, gl, gr, p3, b3, pg, pf, up0, up1, up2,
    r_cot_row, r_cot_tile, r_row, r_strip, r_corner, r_gc_row, r_gc_tile, r_m, r_e,
    shift_sem, send, recv,
):
    device = neighbours()
    barrier = pltpu.get_barrier_semaphore()
    plan = ring_plan(*[None] * 4)
    for dr, dc, _, _ in plan:
        pl.semaphore_signal(barrier, inc=1, device_id=device(dr, dc), device_id_type=MESH)
    shift_copy = pltpu.make_async_copy(shift_hbm, shift_ref, shift_sem)
    shift_copy.start()
    has_up, has_down, has_left, has_right = edge_flags()
    started = []

    def start(stage, plan, targets):
        copies = []
        for dr, dc, source, n in plan:
            copies.append(
                pltpu.make_async_remote_copy(
                    src_ref=source,
                    dst_ref=targets[n],
                    send_sem=send.at[stage, n],
                    recv_sem=recv.at[stage, n],
                    device_id=device(dr, dc),
                    device_id_type=MESH,
                )
            )
            copies[-1].start()
        started.extend(copies)
        return copies

    def arrived(copies):
        for copy in copies:
            copy.wait_recv()

    lane = lanes((C, 128))
    for c in range(C):
        for t in range(2):
            cs[t, pl.ds(c, R, stride=C), :] = cot_ref[0, c, :, t * 128 : t * 128 + 128].astype(F32)
    low = jnp.zeros((C, 128), F32)
    high = jnp.zeros((C, 128), F32)
    for r in range(R):
        at = slice(r * C, r * C + C)
        low = jnp.where(lane == r, roll(cs[0, at, :], r), low)
        high = jnp.where(lane == r, roll(cs[1, at, :], r - 127), high)
    cl[...] = low.astype(BF16)
    cr[...] = high.astype(BF16)
    for t in range(2):
        ct[:, t * 128 : t * 128 + 128] = cs[t].astype(BF16)
    for c in range(C):
        for t in range(2):
            fs[t, pl.ds(c, R, stride=C), :] = feat_ref[0, c, :, t * 128 : t * 128 + 128].astype(F32)
    for t in range(2):
        ft[:, t * 128 : t * 128 + 128] = fs[t].astype(BF16)
    for p in range(5):
        low = jnp.zeros((C, 128), F32)
        high = jnp.zeros((C, 128), F32)
        for g in range(7):
            r = 7 * p + g
            if r < R:
                at = slice(r * C, r * C + C)
                here = (lane >= 18 * g) & (lane < 18 * g + 17)
                low = jnp.where(here, roll(fs[0, at, :], 18 * g), low)
                high = jnp.where(here, roll(fs[1, at, :], 18 * g + 17), high)
        sl[p * C : p * C + C, :] = low.astype(BF16)
        sr[p * C : p * C + C, :] = high.astype(BF16)
    pl.semaphore_wait(barrier, len(plan))
    cot_copies = start(
        0,
        ring_plan(ct.at[0:C, :], ct.at[(R - 1) * C : R * C, :], cl, cr),
        [r_cot_row.at[0], r_cot_row.at[1]] + [r_cot_tile.at[n] for n in range(6)],
    )
    feat_copies = start(
        1,
        ring_plan(
            ft.at[0 : 17 * C, :],
            ft.at[15 * C : R * C, :],
            sl,
            sr,
            sl.at[0:96, :],
            sl.at[64:160, :],
            sr.at[0:96, :],
            sr.at[64:160, :],
        ),
        [r_row.at[0], r_row.at[1], r_strip.at[0], r_strip.at[1]] + [r_corner.at[n] for n in range(4)],
    )

    w2t[...] = banded(backward_taps(k2_ref))
    w1[...] = banded(forward_taps(k1_ref))
    wbt[...] = banded(backward_taps(kb_ref))
    wb[...] = banded(forward_taps(kb_ref))
    w2[...] = banded(forward_taps(k2_ref))
    fe[1, 17 * C : 49 * C, :] = fs[0]
    fe[2, 17 * C : 49 * C, :] = fs[1]
    cell = 32 + lax.shift_right_logical(lax.broadcasted_iota(jnp.int32, (S, 128), 0), 2)
    gather = jnp.where(cell == lanes((S, 128)), 1.0, 0.0).astype(BF16)

    def pooled(value, k, ref, scale):
        sums = jnp.dot(value, gather, preferred_element_type=F32)
        for j in range(2):
            four = sums[j * 128 : j * 128 + 128]
            four = (four[0:32] + four[32:64]) + (four[64:96] + four[96:128])
            at = (2 * k + j) * C
            ref[at : at + C, :] = (four * scale).astype(BF16)

    arrived(cot_copies)
    tiles = [r_cot_tile[n].astype(F32) for n in range(6)]
    for r in range(-1, R + 1):
        if r < 0:
            x = r_cot_row[0].astype(F32) * has_up
            a, b, t, keep = tiles[2], tiles[3], R - 1, has_up
        elif r == R:
            x = r_cot_row[1].astype(F32) * has_down
            a, b, t, keep = tiles[4], tiles[5], 0, has_down
        else:
            x = both_halves(cs, slice(r * C, r * C + C))
            a, b, t, keep = tiles[0], tiles[1], r, 1.0
        store_three(
            c3, r + 1, with_edges(x, roll(a, -t) * (has_left * keep), roll(b, 127 - t) * (has_right * keep))
        )
    for k in range(R // B):
        rows = slice(k * B * C, (k + 1) * B * C)
        depth = slice(k * B * 96, k * B * 96 + K)
        value = jnp.dot(w2t[...], c3[depth, :], preferred_element_type=F32).astype(BF16)
        bg[rows, :] = value
        pooled(value, k, coarse, 1.0)
    low = jnp.zeros((C, 128), F32)
    high = jnp.zeros((C, 128), F32)
    for j in range(8):
        value = coarse[j * C : j * C + C, :].astype(F32)
        low = jnp.where(lane == j, roll(value, j - 32), low)
        high = jnp.where(lane == j, roll(value, j - 95), high)
    gl[...] = low.astype(BF16)
    gr[...] = high.astype(BF16)
    coarse_copies = start(
        2,
        ring_plan(coarse.at[0:C, :], coarse.at[7 * C : 8 * C, :], gl, gr),
        [r_gc_row.at[0], r_gc_row.at[1]] + [r_gc_tile.at[n] for n in range(6)],
    )

    arrived(feat_copies)
    for t in range(2):
        cols = slice(t * 128, t * 128 + 128)
        fe[t + 1, 0 : 17 * C, :] = r_row[0, :, cols].astype(F32) * has_up
        fe[t + 1, 49 * C :, :] = r_row[1, :, cols].astype(F32) * has_down
    for side, mid, above, below, offset, flag in (
        (0, r_strip.at[0], r_corner.at[0], r_corner.at[2], 111, has_left),
        (3, r_strip.at[1], r_corner.at[1], r_corner.at[3], 0, has_right),
    ):
        for r in range(-17, R + 17):
            if r < 0:
                source, their, first, keep = above, r + R, 2, flag * has_up
            elif r >= R:
                source, their, first, keep = below, r - R, 0, flag * has_down
            else:
                source, their, first, keep = mid, r, 0, flag
            at = (their // 7 - first) * C
            value = source[at : at + C, :].astype(F32)
            fe[side, (r + 17) * C : (r + 18) * C, :] = roll(value, offset - 18 * (their % 7)) * keep

    shift_copy.wait()
    for c in range(C):
        row_shift, col_shift = shift_ref[0, c, 0], shift_ref[0, c, 1]
        x = jnp.concatenate(
            [fe[t, pl.ds((M + row_shift) * C + c, R + 2, stride=C), :] for t in range(4)], axis=1
        )
        for b in range(3):
            y = pltpu.roll(x, 385 - b - col_shift, 1)
            for t in range(2):
                xf[t, pl.ds(b * C + c, R + 2, stride=96), :] = y[:, t * 128 : t * 128 + 128]
    wide = lanes((C, S))
    first_lane = jnp.where(wide == 0, has_left, 1.0)
    last_lane = jnp.where(wide == S - 1, has_right, 1.0)
    for row in range(R + 2):
        scale = has_up if row == 0 else has_down if row == R + 1 else None
        for b in range(3):
            at = row * 96 + b * C
            value = both_halves(xf, slice(at, at + C))
            if b != 1:
                value = value * (first_lane if b == 0 else last_lane)
            if scale is not None:
                value = value * scale
            x3[at : at + C, :] = value.astype(BF16)

    for k in range(R // B):
        rows = slice(k * B * C, (k + 1) * B * C)
        depth = slice(k * B * 96, k * B * 96 + K)
        pre = jnp.dot(w1[...], x3[depth, :], preferred_element_type=F32)
        sigma = 1.0 / (1.0 + jnp.exp(-pre))
        value = (pre * sigma).astype(BF16)
        act[rows, :] = value
        slope[rows, :] = sigma * (1.0 + pre * (1.0 - sigma))
        pooled(value, k, pool, 1.0 / 16.0)
    mu[0:32, :] = act[0:32, 0:128]
    mu[32:64, :] = act[0:32, 128:256]
    mu[64:128, :] = pool[0:64, :]
    md[0:32, :] = act[31 * C :, 0:128]
    md[32:64, :] = act[31 * C :, 128:256]
    md[64:128, :] = pool[192:256, :]
    low = jnp.zeros((C, 128), F32)
    high = jnp.zeros((C, 128), F32)
    for j in range(8):
        for v in range(4):
            at = (4 * j + v) * C
            t = 8 * j + v
            low = jnp.where(lane == t, roll(act[at : at + C, 0:128].astype(F32), t), low)
            high = jnp.where(lane == t, roll(act[at : at + C, 128:256].astype(F32), t - 127), high)
        t = 8 * j + 4
        two = (lane == t) | (lane == t + 1)
        value = pool[j * C : j * C + C, :].astype(F32)
        low = jnp.where(two, roll(value, t - 32), low)
        high = jnp.where(two, roll(value, t - 94), high)
    el[...] = low.astype(BF16)
    er[...] = high.astype(BF16)
    edge_copies = start(
        3, ring_plan(mu, md, el, er), [r_m.at[0], r_m.at[1]] + [r_e.at[n] for n in range(6)]
    )

    def cells(width, centre, tile_refs, lane_of):
        left_tiles = [2] * 2 + [0] * 8 + [4] * 2
        for row in range(-width, 8 + width):
            n = left_tiles[row + 2]
            t = lane_of(row % 8)
            x = centre(row).astype(F32)
            left = roll(tile_refs[n].astype(F32), 32 - width - t)
            right = roll(tile_refs[n + 1].astype(F32), 96 - t)
            x = jnp.where((lane >= 32 - width) & (lane < 32), left * has_left, x)
            x = jnp.where((lane >= 96) & (lane < 96 + width), right * has_right, x)
            if row < 0 or row >= 8:
                x = x * (has_up if row < 0 else has_down)
            for b in range(3):
                at = (row + width) * 96 + b * C
                p3[at : at + C, :] = roll(x, 1 - b).astype(BF16)

    def coarse_row(row):
        if row < 0 or row >= 8:
            return r_gc_row[0 if row < 0 else 1]
        return coarse[row * C : row * C + C, :]

    def pooled_row(row):
        if row < 0:
            return r_m[0, 64 + (row + 2) * C : 64 + (row + 3) * C, :]
        if row >= 8:
            return r_m[1, 64 + (row - 8) * C : 64 + (row - 7) * C, :]
        return pool[row * C : row * C + C, :]

    arrived(coarse_copies)
    cells(1, coarse_row, r_gc_tile, lambda j: j)
    grad = jnp.dot(wbt[...], p3[0:K, :], preferred_element_type=F32)
    spread_mid = spread(1)
    up1[0:256, :] = jnp.dot(halves(grad), spread_mid, preferred_element_type=F32) * (1.0 / 16.0)
    for row in range(R):
        at = slice(row * C, row * C + C)
        cell_at = (row // 4) * C
        value = (bg[at, :].astype(F32) + up1[cell_at : cell_at + C, :]) * slope[at, :]
        pg[at, :] = value.astype(BF16)
    total = None
    for k in range(R // B):
        rows = slice(k * B * C, (k + 1) * B * C)
        depth = slice(k * B * 96, k * B * 96 + K)
        part = contract(pg[rows, :], x3[depth, :])
        total = part if total is None else total + part
    first = collected(total, factor)

    arrived(edge_copies)
    cells(2, pooled_row, r_e, lambda j: 8 * j + 4)
    bottle = jnp.concatenate(
        [
            jnp.dot(wb[...], p3[0:K, :], preferred_element_type=F32),
            jnp.dot(wb[...], p3[192 : 192 + K, :], preferred_element_type=F32)[6 * C :],
        ],
        axis=0,
    )
    parts = halves(bottle)
    for b, ref in enumerate((up0, up1, up2)):
        ref[...] = jnp.dot(parts, spread_mid if b == 1 else spread(b), preferred_element_type=F32)

    tiles = [r_e[n].astype(F32) for n in range(6)]
    for row in range(-1, R + 1):
        if row < 0:
            x = jnp.concatenate([r_m[0, 0:32, :], r_m[0, 32:64, :]], axis=1).astype(F32)
            low, high, t = tiles[2], tiles[3], 59
        elif row == R:
            x = jnp.concatenate([r_m[1, 0:32, :], r_m[1, 32:64, :]], axis=1).astype(F32)
            low, high, t = tiles[4], tiles[5], 0
        else:
            x = act[row * C : row * C + C, :].astype(F32)
            low, high, t = tiles[0], tiles[1], 8 * (row // 4) + row % 4
        at = ((row + 4) // 4) * C
        back, mid, ahead = with_edges(x, roll(low, -t), roll(high, 127 - t))
        back = (back + up0[at : at + C, :]) * first_lane
        mid = mid + up1[at : at + C, :]
        ahead = (ahead + up2[at : at + C, :]) * last_lane
        if row < 0 or row == R:
            keep = has_up if row < 0 else has_down
            back, mid, ahead = back * keep, mid * keep, ahead * keep
        store_three(b3, row + 1, (back, mid, ahead))

    total = None
    for k in range(R // B):
        rows = slice(k * B * C, (k + 1) * B * C)
        depth = slice(k * B * 96, k * B * 96 + K)
        part = contract(ct[rows, :], b3[depth, :])
        total = part if total is None else total + part
    second = collected(total, factor)
    both = jnp.concatenate([half(x, t) for t in range(3) for x in (first, second)], axis=0)
    pieces, height = grad_ref.shape[:2]
    for n in range(pieces):
        grad_ref[n] = both[n * height : (n + 1) * height, :]
    for k in range(R // B):
        rows = slice(k * B * C, (k + 1) * B * C)
        depth = slice(k * B * 96, k * B * 96 + K)
        value = jnp.dot(w2[...], b3[depth, :], preferred_element_type=F32)
        pf[0, rows, :] = value[:, 0:128]
        pf[1, rows, :] = value[:, 128:256]
    for o in range(C):
        for t in range(2):
            pred_ref[0, o, :, t * 128 : t * 128 + 128] = pf[t, pl.ds(o, R, stride=C), :].astype(BF16)
    for copy in started:
        copy.wait_send()


def vmem(n):
    return [pl.BlockSpec(memory_space=pltpu.VMEM)] * n


def main(factor, pieces, features, cotangent, shifts, k1, kb, k2):
    def f(*shape):
        return pltpu.VMEM(shape, F32)

    def h(*shape):
        return pltpu.VMEM(shape, BF16)

    scratch = [pltpu.SMEM((1, C, 2), jnp.int32)]
    scratch += [f(2, R * C, 128), f(2, R * C, 128), h(R * C, S), h(R * C, S)]
    scratch += [h(160, 128), h(160, 128), h(C, 128), h(C, 128)]
    scratch += [f(4, 66 * C, 128), f(2, (R + 2) * 96, 128)]
    scratch += [h((R + 2) * 96, S), h((R + 2) * 96, S)] + [h(B * C, K)] * 5
    scratch += [h(R * C, S), f(R * C, S), h(R * C, S), h(256, 128), h(256, 128)]
    scratch += [h(128, 128), h(128, 128)] + [h(C, 128)] * 4
    scratch += [h(12 * 96, 128), h((R + 2) * 96, S), h(R * C, S), f(2, R * C, 128)]
    scratch += [f(10 * C, S)] * 3
    scratch += [h(2, C, S), h(6, C, 128), h(2, 17 * C, S), h(2, 160, 128), h(4, 96, 128)]
    scratch += [h(2, C, 128), h(6, C, 128), h(2, 128, 128), h(6, C, 128)]
    scratch += [pltpu.SemaphoreType.DMA, pltpu.SemaphoreType.DMA((4, 8)), pltpu.SemaphoreType.DMA((4, 8))]
    specs = vmem(6)
    specs[2] = pl.BlockSpec(memory_space=pl.ANY)
    return pl.pallas_call(
        functools.partial(main_kernel, factor),
        out_shape=(
            jax.ShapeDtypeStruct((1, C, R, S), BF16),
            jax.ShapeDtypeStruct((pieces, 192 // pieces, 128), F32),
        ),
        in_specs=specs,
        out_specs=tuple(vmem(2)),
        scratch_shapes=scratch,
        compiler_params=pltpu.CompilerParams(collective_id=0, has_side_effects=True),
        name="main",
    )(features, cotangent, shifts, k1, kb, k2)


def reduce_kernel(grad_ref, first_ref, second_ref, held, mine, column, out_ref, send_a, recv_a, send_b, recv_b, send_c, recv_c):
    row, col, img = lax.axis_index("rows"), lax.axis_index("cols"), lax.axis_index("dp")
    nrows, ncols, ndp = lax.axis_size("rows"), lax.axis_size("cols"), lax.axis_size("dp")
    pieces = ncols * ndp
    me = col * ndp + img

    def peer(d):
        other = lax.rem(me + d, pieces)
        return other, {"cols": other // ndp, "dp": lax.rem(other, ndp)}

    def in_column(d):
        return {"rows": lax.rem(row + d, nrows)}

    barrier = pltpu.get_barrier_semaphore()
    for d in range(1, pieces):
        pl.semaphore_signal(barrier, inc=1, device_id=peer(d)[1], device_id_type=MESH)
    for d in range(1, nrows):
        pl.semaphore_signal(barrier, inc=1, device_id=in_column(d), device_id_type=MESH)
    pl.semaphore_wait(barrier, pieces + nrows - 2)

    copies = []
    for d in range(1, pieces):
        other, device = peer(d)
        copies.append(
            pltpu.make_async_remote_copy(
                src_ref=grad_ref.at[other],
                dst_ref=held.at[d],
                send_sem=send_a.at[d],
                recv_sem=recv_a.at[d],
                device_id=device,
                device_id_type=MESH,
            )
        )
        copies[-1].start()
    total = grad_ref[me]
    for d in range(1, pieces):
        copies[d - 1].wait_recv()
        total = total + held[d]
    mine[...] = total
    column[row] = total
    for d in range(1, nrows):
        copies.append(
            pltpu.make_async_remote_copy(
                src_ref=mine,
                dst_ref=column.at[row],
                send_sem=send_b.at[d],
                recv_sem=recv_b.at[d],
                device_id=in_column(d),
                device_id_type=MESH,
            )
        )
        copies[-1].start()
    for d in range(1, nrows):
        copies[pieces - 2 + d].wait_recv()
    total = column[0]
    for n in range(1, nrows):
        total = total + column[n]
    out_ref[me] = total
    for d in range(1, pieces):
        copies.append(
            pltpu.make_async_remote_copy(
                src_ref=out_ref.at[me],
                dst_ref=out_ref.at[me],
                send_sem=send_c.at[d],
                recv_sem=recv_c.at[d],
                device_id=peer(d)[1],
                device_id_type=MESH,
            )
        )
        copies[-1].start()
    for d in range(1, pieces):
        copies[pieces + nrows - 3 + d].wait_recv()
    whole = jnp.concatenate([out_ref[n] for n in range(pieces)], axis=0)
    for t in range(9):
        for n, ref in enumerate((first_ref, second_ref)):
            at = (t // 4) * 64 + n * C
            ref[t] = roll(whole[at : at + C, :], -32 * (t % 4))[:, 0:C]
    for copy in copies:
        copy.wait_send()


def reduce_all(grads):
    pieces, height = grads.shape[:2]
    nrows = lax.axis_size("rows")
    piece = pltpu.VMEM((height, 128), F32)
    return pl.pallas_call(
        reduce_kernel,
        out_shape=(jax.ShapeDtypeStruct((9, C, C), F32),) * 2,
        in_specs=vmem(1),
        out_specs=tuple(vmem(2)),
        scratch_shapes=[
            pltpu.VMEM((pieces, height, 128), F32),
            piece,
            pltpu.VMEM((nrows, height, 128), F32),
            pltpu.VMEM((pieces, height, 128), F32),
        ]
        + [pltpu.SemaphoreType.DMA((n,)) for n in (pieces, pieces, nrows, nrows, pieces, pieces)],
        compiler_params=pltpu.CompilerParams(collective_id=2, has_side_effects=True),
        name="reduce_all",
    )(grads)


def shards(features, shifts, first_kernel, bottle_kernel, second_kernel, cotangent):
    nrows, ncols, ndp = lax.axis_size("rows"), lax.axis_size("cols"), lax.axis_size("dp")
    assert features.shape == (1, C, R, S)
    factor = 1.0 / math.sqrt(ndp * nrows * R * ncols * S)
    prediction, grads = main(
        factor, ncols * ndp, features, cotangent, shifts, first_kernel, bottle_kernel, second_kernel
    )
    first, second = reduce_all(grads)
    return prediction, first, second


def solution(mesh):
    placed = (
        P("dp", None, "rows", "cols"),
        P("dp", None, None),
        P(),
        P(),
        P(),
        P("dp", None, "rows", "cols"),
    )
    return jax.shard_map(
        shards,
        mesh=mesh,
        in_specs=placed,
        out_specs=(P("dp", None, "rows", "cols"), P(), P()),
        check_vma=False,
    )
```

time: 601 us -> 69.6 us (0.12)
  waiting for transfers between devices: 318 us -> 0 us
  local copies, waits for them, and re-layouts: 149 us -> 4.9 us
  starting transfers between devices: 74.9 us -> 0 us
  Pallas kernels: 0 us -> 63.9 us
  matrix products: 25.9 us -> 0 us
  between operations: 14.9 us -> 0.66 us
  other arithmetic: 13.1 us -> 0 us
    psum x1 -> x0, waiting for transfers between devices: 255 us -> none  [shards(): lax.psum((first_grad, second_grad), ('rows', 'cols', 'dp'))]
    gather x96 -> x0, local copies, waits for them, and re-layouts: 112 us -> none
    ppermute x24 -> x0, starting transfers between devices: 74.8 us -> none  [the longest x12 58.8 us: padded(): lax.ppermute(lax.slice_in_dim(block, block.shape[dim] - width, None, axis...]
    pallas_call x0 -> x2, Pallas kernels: none -> 63.9 us  [the longest x1 39.2 us: main(): pl.pallas_call(functools.partial(main_kernel, factor), out_shape=(jax.Sha...]
    ppermute x24 -> x0, waiting for transfers between devices: 62.9 us -> none  [the longest x12 38.3 us: padded(): lax.ppermute(lax.slice_in_dim(block, 0, width, axis=dim), axis, backward)]
    dot_general x63 -> x0, matrix products: 25.9 us -> none  [the longest x27 10.8 us: convolve_ext(): jnp.einsum('oi,bihw->bohw', kernel[tap_index], window, preferred_element_...]
    broadcast_in_dim x6 -> x0, local copies, waits for them, and re-layouts: 13 us -> none  [upsample(): return jnp.repeat(jnp.repeat(values, POOL, axis=2), POOL, axis=3)]
    reduce_sum x2 -> x0, other arithmetic: 7.2 us -> none  [pool_sum(): values.reshape(shape[0], shape[1], shape[2] // POOL, POOL, shape[3] // PO...]
  transfers between devices with their start and end apart: 25 -> 0, of which waited for: 13 -> 0; matrix products, arithmetic and copies ran while one was open for 5% -> 0% of each run, Pallas kernels for 0% -> 0%
where the time goes in v2:
time: 69.6 us; the launch traced here: 69.5 us
  Pallas kernels  63.9 us (92%)
  local copies, waits for them, and re-layouts  4.9 us (7%)
    pallas_call x1, Pallas kernels, main(): pl.pallas_call(functools.partial(main_kernel, factor), out_shape=(jax.Sha...  39.2 us
    pallas_call x1, Pallas kernels, reduce_all(): pl.pallas_call(reduce_kernel, out_shape=(jax.ShapeDtypeStruct((9, C, C),...  24.7 us
    unnamed x8, local copies, waits for them, and re-layouts  4.9 us

profile of v2, /device:TPU:1, one launch (start us, length us, event | category | flops | bytes accessed | tf_op | source)
XLA Modules:
  0.0 69.5 jit_solution(383418789525775803)
XLA Ops:
  0.6 1.4 %copy.9.shift_hbm = s32[1,32,2]{2,1,0:T(8,128)} copy(s32[1,32,2]{1,2,0:T(2,128)} %param.7) | data formatting | bytes 512 | tf_op args[1]
  2.0 39.2 %main.1 = (bf16[1,32,32,256]{3,2,1,0:T(8,128)(2,1)}, f32[16,12,128]{2,1,0:T(8,128)}) custom-call(bf16[1,32,32,256]{3,2,1,0:T(8,128)(2,1)} %feat_ref.1, bf16[1,32,32,256]{3,2,1,0:T(8,128)(2,1)} %cot_ref.1, s32[1,32,2]{2,1,0:T(8,128)} %copy.9.shift_hbm, bf16[9,32,32]{2,1,0:T(8,128)(2,1)} %k1_ref.1, bf16[9,32,32]{2,1,0:T(8,128)(2,1)} %kb_ref.1, ...), custom_call_target="tpu_custom_call" | custom-call | tf_op jit(solution)/shard_map/main/pallas_call | solution.py:479
  41.2 24.7 %reduce_all.1 = (f32[9,32,32]{2,1,0:T(8,128)}, f32[9,32,32]{2,1,0:T(8,128)}) custom-call(f32[16,12,128]{2,1,0:T(8,128)} %get-tuple-element.8.grad_ref), custom_call_target="tpu_custom_call" | custom-call | tf_op jit(solution)/shard_map/reduce_all/pallas_call | solution.py:578
  65.9 0.0 copy-start.1
  65.9 1.9 %copy.13 = bf16[1,32,32,256]{3,2,1,0:T(8,128)(2,1)} copy(bf16[1,32,32,256]{3,2,1,0:T(8,128)(2,1)} %get-tuple-element.14) | data formatting | bytes 1048576
  67.8 0.0 copy-done.1
  67.8 0.0 copy-start
  67.8 0.7 copy.14
  68.5 0.3 copy-done
  68.8 0.7 copy.15
Async XLA Ops:
  65.9 1.9 %copy-start.1 = (f32[9,32,32]{2,1,0:T(8,128)S(1)}, f32[9,32,32]{2,1,0:T(8,128)}, u32[]{:S(2)}) copy-start(f32[9,32,32]{2,1,0:T(8,128)} %get-tuple-element.15) | copy-start | bytes 110596
  67.8 1.0 %copy-start = (f32[9,32,32]{2,1,0:T(8,128)S(1)}, f32[9,32,32]{2,1,0:T(8,128)}, u32[]{:S(2)}) copy-start(f32[9,32,32]{2,1,0:T(8,128)} %get-tuple-element.16) | copy-start | bytes 110596

commit v3 on v2

--- a/solution.py
+++ b/solution.py
@@ -126,20 +126,32 @@
 
 def main_kernel(
     factor,
-    feat_ref, cot_ref, shift_hbm, k1_ref, kb_ref, k2_ref,
-    pred_ref, grad_ref,
-    shift_ref, fs, cs, ft, ct, sl, sr, cl, cr, fe, xf, x3, c3, w1, w2, w2t, wb, wbt,
+    feat_ref, cot_ref, shift_ref, k1_ref, kb_ref, k2_ref,
+    pred_ref, out_ref,
+    fs, cs, ft, ct, sl, sr, cl, cr, fe, xf, x3, c3, w1, w2, w2t, wb, wbt,
     act, slope, bg, pool, coarse, mu, md, el, er, gl, gr, p3, b3, pg, pf, up0, up1, up2,
     r_cot_row, r_cot_tile, r_row, r_strip, r_corner, r_gc_row, r_gc_tile, r_m, r_e,
-    shift_sem, send, recv,
+    grad_ref, held, mine, column,
+    send, recv, send_a, recv_a, send_b, recv_b, send_c, recv_c,
 ):
     device = neighbours()
+    my_row, col, img = lax.axis_index("rows"), lax.axis_index("cols"), lax.axis_index("dp")
+    nrows, ncols, ndp = lax.axis_size("rows"), lax.axis_size("cols"), lax.axis_size("dp")
+    pieces = ncols * ndp
+    me = col * ndp + img
+
+    def peer(d):
+        other = lax.rem(me + d, pieces)
+        return other, {"cols": other // ndp, "dp": lax.rem(other, ndp)}
+
+    def in_column(d):
+        return {"rows": lax.rem(my_row + d, nrows)}
+
     barrier = pltpu.get_barrier_semaphore()
-    plan = ring_plan(*[None] * 4)
-    for dr, dc, _, _ in plan:
-        pl.semaphore_signal(barrier, inc=1, device_id=device(dr, dc), device_id_type=MESH)
-    shift_copy = pltpu.make_async_copy(shift_hbm, shift_ref, shift_sem)
-    shift_copy.start()
+    greeted = [device(dr, dc) for dr in (-1, 1) for dc in (-1, 1)]
+    greeted += [in_column(d) for d in range(1, nrows)] + [peer(d)[1] for d in range(1, pieces)]
+    for other in greeted:
+        pl.semaphore_signal(barrier, inc=1, device_id=other, device_id_type=MESH)
     has_up, has_down, has_left, has_right = edge_flags()
     started = []
 
@@ -195,7 +207,7 @@
                 high = jnp.where(here, roll(fs[1, at, :], 18 * g + 17), high)
         sl[p * C : p * C + C, :] = low.astype(BF16)
         sr[p * C : p * C + C, :] = high.astype(BF16)
-    pl.semaphore_wait(barrier, len(plan))
+    pl.semaphore_wait(barrier, len(greeted))
     cot_copies = start(
         0,
         ring_plan(ct.at[0:C, :], ct.at[(R - 1) * C : R * C, :], cl, cr),
@@ -289,9 +301,8 @@
             value = source[at : at + C, :].astype(F32)
             fe[side, (r + 17) * C : (r + 18) * C, :] = roll(value, offset - 18 * (their % 7)) * keep
 
-    shift_copy.wait()
     for c in range(C):
-        row_shift, col_shift = shift_ref[0, c, 0], shift_ref[0, c, 1]
+        row_shift, col_shift = shift_ref[0, 0, c], shift_ref[0, 1, c]
         x = jnp.concatenate(
             [fe[t, pl.ds((M + row_shift) * C + c, R + 2, stride=C), :] for t in range(4)], axis=1
         )
@@ -435,18 +446,54 @@
         total = part if total is None else total + part
     second = collected(total, factor)
     both = jnp.concatenate([half(x, t) for t in range(3) for x in (first, second)], axis=0)
-    pieces, height = grad_ref.shape[:2]
+    height = grad_ref.shape[1]
     for n in range(pieces):
         grad_ref[n] = both[n * height : (n + 1) * height, :]
+
+    def send_to(device_id, source, target, send_sem, recv_sem):
+        copy = pltpu.make_async_remote_copy(
+            src_ref=source,
+            dst_ref=target,
+            send_sem=send_sem,
+            recv_sem=recv_sem,
+            device_id=device_id,
+            device_id_type=MESH,
+        )
+        copy.start()
+        started.append(copy)
+        return copy
+
+    copies = []
+    for d in range(1, pieces):
+        other, device_id = peer(d)
+        copies.append(send_to(device_id, grad_ref.at[other], held.at[d], send_a.at[d], recv_a.at[d]))
     for k in range(R // B):
         rows = slice(k * B * C, (k + 1) * B * C)
         depth = slice(k * B * 96, k * B * 96 + K)
         value = jnp.dot(w2[...], b3[depth, :], preferred_element_type=F32)
         pf[0, rows, :] = value[:, 0:128]
         pf[1, rows, :] = value[:, 128:256]
+    arrived(copies)
+    total = grad_ref[me]
+    for d in range(1, pieces):
+        total = total + held[d]
+    mine[...] = total
+    column[my_row] = total
+    copies = []
+    for d in range(1, nrows):
+        copies.append(send_to(in_column(d), mine, column.at[my_row], send_b.at[d], recv_b.at[d]))
     for o in range(C):
         for t in range(2):
             pred_ref[0, o, :, t * 128 : t * 128 + 128] = pf[t, pl.ds(o, R, stride=C), :].astype(BF16)
+    arrived(copies)
+    total = column[0]
+    for n in range(1, nrows):
+        total = total + column[n]
+    out_ref[me] = total
+    copies = []
+    for d in range(1, pieces):
+        copies.append(send_to(peer(d)[1], out_ref.at[me], out_ref.at[me], send_c.at[d], recv_c.at[d]))
+    arrived(copies)
     for copy in started:
         copy.wait_send()
 
@@ -462,8 +509,8 @@
     def h(*shape):
         return pltpu.VMEM(shape, BF16)
 
-    scratch = [pltpu.SMEM((1, C, 2), jnp.int32)]
-    scratch += [f(2, R * C, 128), f(2, R * C, 128), h(R * C, S), h(R * C, S)]
+    height, nrows = 192 // pieces, lax.axis_size("rows")
+    scratch = [f(2, R * C, 128), f(2, R * C, 128), h(R * C, S), h(R * C, S)]
     scratch += [h(160, 128), h(160, 128), h(C, 128), h(C, 128)]
     scratch += [f(4, 66 * C, 128), f(2, (R + 2) * 96, 128)]
     scratch += [h((R + 2) * 96, S), h((R + 2) * 96, S)] + [h(B * C, K)] * 5
@@ -473,9 +520,11 @@
     scratch += [f(10 * C, S)] * 3
     scratch += [h(2, C, S), h(6, C, 128), h(2, 17 * C, S), h(2, 160, 128), h(4, 96, 128)]
     scratch += [h(2, C, 128), h(6, C, 128), h(2, 128, 128), h(6, C, 128)]
-    scratch += [pltpu.SemaphoreType.DMA, pltpu.SemaphoreType.DMA((4, 8)), pltpu.SemaphoreType.DMA((4, 8))]
+    scratch += [f(pieces, height, 128), f(pieces, height, 128), f(height, 128), f(nrows, height, 128)]
+    scratch += [pltpu.SemaphoreType.DMA((4, 8)), pltpu.SemaphoreType.DMA((4, 8))]
+    scratch += [pltpu.SemaphoreType.DMA((n,)) for n in (pieces, pieces, nrows, nrows, pieces, pieces)]
     specs = vmem(6)
-    specs[2] = pl.BlockSpec(memory_space=pl.ANY)
+    specs[2] = pl.BlockSpec(memory_space=pltpu.SMEM)
     return pl.pallas_call(
         functools.partial(main_kernel, factor),
         out_shape=(
@@ -490,106 +539,24 @@
     )(features, cotangent, shifts, k1, kb, k2)
 
 
-def reduce_kernel(grad_ref, first_ref, second_ref, held, mine, column, out_ref, send_a, recv_a, send_b, recv_b, send_c, recv_c):
-    row, col, img = lax.axis_index("rows"), lax.axis_index("cols"), lax.axis_index("dp")
-    nrows, ncols, ndp = lax.axis_size("rows"), lax.axis_size("cols"), lax.axis_size("dp")
-    pieces = ncols * ndp
-    me = col * ndp + img
-
-    def peer(d):
-        other = lax.rem(me + d, pieces)
-        return other, {"cols": other // ndp, "dp": lax.rem(other, ndp)}
-
-    def in_column(d):
-        return {"rows": lax.rem(row + d, nrows)}
-
-    barrier = pltpu.get_barrier_semaphore()
-    for d in range(1, pieces):
-        pl.semaphore_signal(barrier, inc=1, device_id=peer(d)[1], device_id_type=MESH)
-    for d in range(1, nrows):
-        pl.semaphore_signal(barrier, inc=1, device_id=in_column(d), device_id_type=MESH)
-    pl.semaphore_wait(barrier, pieces + nrows - 2)
-
-    copies = []
-    for d in range(1, pieces):
-        other, device = peer(d)
-        copies.append(
-            pltpu.make_async_remote_copy(
-                src_ref=grad_ref.at[other],
-                dst_ref=held.at[d],
-                send_sem=send_a.at[d],
-                recv_sem=recv_a.at[d],
-                device_id=device,
-                device_id_type=MESH,
-            )
-        )
-        copies[-1].start()
-    total = grad_ref[me]
-    for d in range(1, pieces):
-        copies[d - 1].wait_recv()
-        total = total + held[d]
-    mine[...] = total
-    column[row] = total
-    for d in range(1, nrows):
-        copies.append(
-            pltpu.make_async_remote_copy(
-                src_ref=mine,
-                dst_ref=column.at[row],
-                send_sem=send_b.at[d],
-                recv_sem=recv_b.at[d],
-                device_id=in_column(d),
-                device_id_type=MESH,
-            )
-        )
-        copies[-1].start()
-    for d in range(1, nrows):
-        copies[pieces - 2 + d].wait_recv()
-    total = column[0]
-    for n in range(1, nrows):
-        total = total + column[n]
-    out_ref[me] = total
-    for d in range(1, pieces):
-        copies.append(
-            pltpu.make_async_remote_copy(
-                src_ref=out_ref.at[me],
-                dst_ref=out_ref.at[me],
-                send_sem=send_c.at[d],
-                recv_sem=recv_c.at[d],
-                device_id=peer(d)[1],
-                device_id_type=MESH,
-            )
-        )
-        copies[-1].start()
-    for d in range(1, pieces):
-        copies[pieces + nrows - 3 + d].wait_recv()
-    whole = jnp.concatenate([out_ref[n] for n in range(pieces)], axis=0)
+def finish_kernel(pred_ref, sums_ref, out_ref, first_ref, second_ref):
+    out_ref[...] = pred_ref[...]
+    whole = jnp.concatenate([sums_ref[n] for n in range(sums_ref.shape[0])], axis=0)
     for t in range(9):
         for n, ref in enumerate((first_ref, second_ref)):
             at = (t // 4) * 64 + n * C
             ref[t] = roll(whole[at : at + C, :], -32 * (t % 4))[:, 0:C]
-    for copy in copies:
-        copy.wait_send()
-
-
-def reduce_all(grads):
-    pieces, height = grads.shape[:2]
-    nrows = lax.axis_size("rows")
-    piece = pltpu.VMEM((height, 128), F32)
+
+
+def finish(prediction, sums):
     return pl.pallas_call(
-        reduce_kernel,
-        out_shape=(jax.ShapeDtypeStruct((9, C, C), F32),) * 2,
-        in_specs=vmem(1),
-        out_specs=tuple(vmem(2)),
-        scratch_shapes=[
-            pltpu.VMEM((pieces, height, 128), F32),
-            piece,
-            pltpu.VMEM((nrows, height, 128), F32),
-            pltpu.VMEM((pieces, height, 128), F32),
-        ]
-        + [pltpu.SemaphoreType.DMA((n,)) for n in (pieces, pieces, nrows, nrows, pieces, pieces)],
-        compiler_params=pltpu.CompilerParams(collective_id=2, has_side_effects=True),
-        name="reduce_all",
-    )(grads)
+        finish_kernel,
+        out_shape=(jax.ShapeDtypeStruct(prediction.shape, BF16),)
+        + (jax.ShapeDtypeStruct((9, C, C), F32),) * 2,
+        in_specs=vmem(2),
+        out_specs=tuple(vmem(3)),
+        name="finish",
+    )(prediction, sums)
 
 
 def shards(features, shifts, first_kernel, bottle_kernel, second_kernel, cotangent):
@@ -597,10 +564,9 @@
     assert features.shape == (1, C, R, S)
     factor = 1.0 / math.sqrt(ndp * nrows * R * ncols * S)
     prediction, grads = main(
-        factor, ncols * ndp, features, cotangent, shifts, first_kernel, bottle_kernel, second_kernel
-    )
-    first, second = reduce_all(grads)
-    return prediction, first, second
+        factor, ncols * ndp, features, cotangent, shifts.transpose(0, 2, 1), first_kernel, bottle_kernel, second_kernel
+    )
+    return finish(prediction, grads)
 
 
 def solution(mesh):

time: 69.6 us -> 60.2 us (0.86)
  local copies, waits for them, and re-layouts: 4.9 us -> 0 us
  Pallas kernels: 63.9 us -> 59.4 us
    pallas_call x1, Pallas kernels: 24.7 us -> 2 us  [finish(): pl.pallas_call(finish_kernel, out_shape=(jax.ShapeDtypeStruct(prediction....]
    pallas_call x1, Pallas kernels: 39.2 us -> 57.4 us  [main(): pl.pallas_call(functools.partial(main_kernel, factor), out_shape=(jax.Sha...]
    unnamed x8 -> x0, local copies, waits for them, and re-layouts: 4.9 us -> none
where the time goes in v3:
time: 60.2 us; the launch traced here: 60 us
  Pallas kernels  59.4 us (99%)
  between operations  0.64 us (1%)
    pallas_call x1, Pallas kernels, main(): pl.pallas_call(functools.partial(main_kernel, factor), out_shape=(jax.Sha...  57.4 us
    pallas_call x1, Pallas kernels, finish(): pl.pallas_call(finish_kernel, out_shape=(jax.ShapeDtypeStruct(prediction....  2 us

profile of v3, /device:TPU:1, one launch (start us, length us, event | category | flops | bytes accessed | tf_op | source)
XLA Modules:
  0.0 60.0 jit_solution(1741789508631204428)
XLA Ops:
  0.6 57.4 %main.1 = (bf16[1,32,32,256]{3,2,1,0:T(8,128)(2,1)}, f32[16,12,128]{2,1,0:T(8,128)}) custom-call(bf16[1,32,32,256]{3,2,1,0:T(8,128)(2,1)} %feat_ref.1, bf16[1,32,32,256]{3,2,1,0:T(8,128)(2,1)} %cot_ref.1, s32[1,2,32]{2,1,0:T(2,128)} %bitcast.1, bf16[9,32,32]{2,1,0:T(8,128)(2,1)} %k1_ref.1, bf16[9,32,32]{2,1,0:T(8,128)(2,1)} %kb_ref.1, bf16[9,32,32]{2,1,0:T(8,128)(2,1)} %k2_ref.1), custom_call_target="tpu_custom_call" | custom-call | tf_op jit(solution)/shard_map/main/pallas_call | solution.py:528
  58.0 2.0 %finish.1 = (bf16[1,32,32,256]{3,2,1,0:T(8,128)(2,1)}, f32[9,32,32]{2,1,0:T(8,128)}, f32[9,32,32]{2,1,0:T(8,128)}) custom-call(bf16[1,32,32,256]{3,2,1,0:T(8,128)(2,1)} %get-tuple-element.5.pred_ref, f32[16,12,128]{2,1,0:T(8,128)} %get-tuple-element.6.sums_ref), custom_call_target="tpu_custom_call" | custom-call | tf_op jit(solution)/shard_map/finish/pallas_call | solution.py:552

commit v4 on v3

--- a/solution.py
+++ b/solution.py
@@ -14,6 +14,7 @@
 M = 16
 B = 8
 K = (B + 2) * 3 * C
+PITCH = C + 1
 F32 = jnp.float32
 BF16 = jnp.bfloat16
 MESH = pl.DeviceIdType.MESH
@@ -128,7 +129,7 @@
     factor,
     feat_ref, cot_ref, shift_ref, k1_ref, kb_ref, k2_ref,
     pred_ref, out_ref,
-    fs, cs, ft, ct, sl, sr, cl, cr, fe, xf, x3, c3, w1, w2, w2t, wb, wbt,
+    ft, ct, sl, sr, cl, cr, fe, xf, x3, c3, w1, w2, w2t, wb, wbt,
     act, slope, bg, pool, coarse, mu, md, el, er, gl, gr, p3, b3, pg, pf, up0, up1, up2,
     r_cot_row, r_cot_tile, r_row, r_strip, r_corner, r_gc_row, r_gc_tile, r_m, r_e,
     grad_ref, held, mine, column,
@@ -177,36 +178,28 @@
             copy.wait_recv()
 
     lane = lanes((C, 128))
-    for c in range(C):
-        for t in range(2):
-            cs[t, pl.ds(c, R, stride=C), :] = cot_ref[0, c, :, t * 128 : t * 128 + 128].astype(F32)
-    low = jnp.zeros((C, 128), F32)
-    high = jnp.zeros((C, 128), F32)
+    ct[...] = jnp.transpose(cot_ref[0], (1, 0, 2)).reshape(R * C, S)
+    low = jnp.zeros((C, 128), BF16)
+    high = jnp.zeros((C, 128), BF16)
     for r in range(R):
         at = slice(r * C, r * C + C)
-        low = jnp.where(lane == r, roll(cs[0, at, :], r), low)
-        high = jnp.where(lane == r, roll(cs[1, at, :], r - 127), high)
-    cl[...] = low.astype(BF16)
-    cr[...] = high.astype(BF16)
-    for t in range(2):
-        ct[:, t * 128 : t * 128 + 128] = cs[t].astype(BF16)
-    for c in range(C):
-        for t in range(2):
-            fs[t, pl.ds(c, R, stride=C), :] = feat_ref[0, c, :, t * 128 : t * 128 + 128].astype(F32)
-    for t in range(2):
-        ft[:, t * 128 : t * 128 + 128] = fs[t].astype(BF16)
+        low = jnp.where(lane == r, roll(ct[at, 0:128], r), low)
+        high = jnp.where(lane == r, roll(ct[at, 128:256], r - 127), high)
+    cl[...] = low
+    cr[...] = high
+    ft[...] = jnp.transpose(feat_ref[0], (1, 0, 2)).reshape(R * C, S)
     for p in range(5):
-        low = jnp.zeros((C, 128), F32)
-        high = jnp.zeros((C, 128), F32)
+        low = jnp.zeros((C, 128), BF16)
+        high = jnp.zeros((C, 128), BF16)
         for g in range(7):
             r = 7 * p + g
             if r < R:
                 at = slice(r * C, r * C + C)
                 here = (lane >= 18 * g) & (lane < 18 * g + 17)
-                low = jnp.where(here, roll(fs[0, at, :], 18 * g), low)
-                high = jnp.where(here, roll(fs[1, at, :], 18 * g + 17), high)
-        sl[p * C : p * C + C, :] = low.astype(BF16)
-        sr[p * C : p * C + C, :] = high.astype(BF16)
+                low = jnp.where(here, roll(ft[at, 0:128], 18 * g), low)
+                high = jnp.where(here, roll(ft[at, 128:256], 18 * g + 17), high)
+        sl[p * C : p * C + C, :] = low
+        sr[p * C : p * C + C, :] = high
     pl.semaphore_wait(barrier, len(greeted))
     cot_copies = start(
         0,
@@ -233,8 +226,10 @@
     wbt[...] = banded(backward_taps(kb_ref))
     wb[...] = banded(forward_taps(kb_ref))
     w2[...] = banded(forward_taps(k2_ref))
-    fe[1, 17 * C : 49 * C, :] = fs[0]
-    fe[2, 17 * C : 49 * C, :] = fs[1]
+    for r in range(R):
+        for t in range(2):
+            at = (r + 17) * PITCH
+            fe[t + 1, at : at + C, :] = ft[r * C : r * C + C, t * 128 : t * 128 + 128].astype(F32)
     cell = 32 + lax.shift_right_logical(lax.broadcasted_iota(jnp.int32, (S, 128), 0), 2)
     gather = jnp.where(cell == lanes((S, 128)), 1.0, 0.0).astype(BF16)
 
@@ -247,34 +242,37 @@
             ref[at : at + C, :] = (four * scale).astype(BF16)
 
     arrived(cot_copies)
-    tiles = [r_cot_tile[n].astype(F32) for n in range(6)]
+    tiles = [r_cot_tile[n] for n in range(6)]
+    left_flag, right_flag = has_left.astype(BF16), has_right.astype(BF16)
+    up_flag, down_flag = has_up.astype(BF16), has_down.astype(BF16)
     for r in range(-1, R + 1):
         if r < 0:
-            x = r_cot_row[0].astype(F32) * has_up
-            a, b, t, keep = tiles[2], tiles[3], R - 1, has_up
+            x = r_cot_row[0] * up_flag
+            a, b, t, keep = tiles[2], tiles[3], R - 1, up_flag
         elif r == R:
-            x = r_cot_row[1].astype(F32) * has_down
-            a, b, t, keep = tiles[4], tiles[5], 0, has_down
+            x = r_cot_row[1] * down_flag
+            a, b, t, keep = tiles[4], tiles[5], 0, down_flag
         else:
-            x = both_halves(cs, slice(r * C, r * C + C))
-            a, b, t, keep = tiles[0], tiles[1], r, 1.0
-        store_three(
-            c3, r + 1, with_edges(x, roll(a, -t) * (has_left * keep), roll(b, 127 - t) * (has_right * keep))
-        )
+            x = ct[r * C : r * C + C, :]
+            a, b, t, keep = tiles[0], tiles[1], r, None
+        a, b = roll(a, -t) * left_flag, roll(b, 127 - t) * right_flag
+        if keep is not None:
+            a, b = a * keep, b * keep
+        store_three(c3, r + 1, with_edges(x, a, b))
     for k in range(R // B):
         rows = slice(k * B * C, (k + 1) * B * C)
         depth = slice(k * B * 96, k * B * 96 + K)
         value = jnp.dot(w2t[...], c3[depth, :], preferred_element_type=F32).astype(BF16)
         bg[rows, :] = value
         pooled(value, k, coarse, 1.0)
-    low = jnp.zeros((C, 128), F32)
-    high = jnp.zeros((C, 128), F32)
+    low = jnp.zeros((C, 128), BF16)
+    high = jnp.zeros((C, 128), BF16)
     for j in range(8):
-        value = coarse[j * C : j * C + C, :].astype(F32)
+        value = coarse[j * C : j * C + C, :]
         low = jnp.where(lane == j, roll(value, j - 32), low)
         high = jnp.where(lane == j, roll(value, j - 95), high)
-    gl[...] = low.astype(BF16)
-    gr[...] = high.astype(BF16)
+    gl[...] = low
+    gr[...] = high
     coarse_copies = start(
         2,
         ring_plan(coarse.at[0:C, :], coarse.at[7 * C : 8 * C, :], gl, gr),
@@ -284,8 +282,12 @@
     arrived(feat_copies)
     for t in range(2):
         cols = slice(t * 128, t * 128 + 128)
-        fe[t + 1, 0 : 17 * C, :] = r_row[0, :, cols].astype(F32) * has_up
-        fe[t + 1, 49 * C :, :] = r_row[1, :, cols].astype(F32) * has_down
+        for r in range(17):
+            rows = slice(r * C, r * C + C)
+            at = r * PITCH
+            fe[t + 1, at : at + C, :] = r_row[0, rows, cols].astype(F32) * has_up
+            at = (r + 49) * PITCH
+            fe[t + 1, at : at + C, :] = r_row[1, rows, cols].astype(F32) * has_down
     for side, mid, above, below, offset, flag in (
         (0, r_strip.at[0], r_corner.at[0], r_corner.at[2], 111, has_left),
         (3, r_strip.at[1], r_corner.at[1], r_corner.at[3], 0, has_right),
@@ -299,30 +301,39 @@
                 source, their, first, keep = mid, r, 0, flag
             at = (their // 7 - first) * C
             value = source[at : at + C, :].astype(F32)
-            fe[side, (r + 17) * C : (r + 18) * C, :] = roll(value, offset - 18 * (their % 7)) * keep
-
+            fe[side, (r + 17) * PITCH : (r + 17) * PITCH + C, :] = roll(value, offset - 18 * (their % 7)) * keep
+
+    long_lane = lanes((R + 2, 128))
     for c in range(C):
         row_shift, col_shift = shift_ref[0, 0, c], shift_ref[0, 1, c]
-        x = jnp.concatenate(
-            [fe[t, pl.ds((M + row_shift) * C + c, R + 2, stride=C), :] for t in range(4)], axis=1
+        turn = lax.rem(128 - col_shift, 128)
+        turned = [
+            pltpu.roll(fe[t, pl.ds((M + row_shift) * PITCH + c, R + 2, stride=PITCH), :], turn, 1)
+            for t in range(4)
+        ]
+        before = long_lane + col_shift < 0
+        after = long_lane + col_shift >= 128
+        rows = pl.ds(c, R + 2, stride=PITCH)
+        for t in range(2):
+            xf[t, rows, :] = jnp.where(before, turned[t], jnp.where(after, turned[t + 2], turned[t + 1]))
+        xf[2, rows, :] = jnp.where(
+            long_lane >= 64,
+            jnp.where(after, turned[1], turned[0]),
+            jnp.where(before, turned[2], turned[3]),
         )
-        for b in range(3):
-            y = pltpu.roll(x, 385 - b - col_shift, 1)
-            for t in range(2):
-                xf[t, pl.ds(b * C + c, R + 2, stride=96), :] = y[:, t * 128 : t * 128 + 128]
     wide = lanes((C, S))
     first_lane = jnp.where(wide == 0, has_left, 1.0)
     last_lane = jnp.where(wide == S - 1, has_right, 1.0)
+    edge_lane = jnp.where(lane >= 64, has_left, has_right)
     for row in range(R + 2):
-        scale = has_up if row == 0 else has_down if row == R + 1 else None
-        for b in range(3):
-            at = row * 96 + b * C
-            value = both_halves(xf, slice(at, at + C))
-            if b != 1:
-                value = value * (first_lane if b == 0 else last_lane)
-            if scale is not None:
-                value = value * scale
-            x3[at : at + C, :] = value.astype(BF16)
+        at = slice(row * PITCH, row * PITCH + C)
+        x = both_halves(xf, at)
+        edge = xf[2, at, :] * edge_lane
+        if row == 0 or row == R + 1:
+            keep = has_up if row == 0 else has_down
+            x, edge = x * keep, edge * keep
+        edge = edge.astype(BF16)
+        store_three(x3, row, with_edges(x.astype(BF16), roll(edge, 1), roll(edge, 127)))
 
     for k in range(R // B):
         rows = slice(k * B * C, (k + 1) * B * C)
@@ -339,21 +350,21 @@
     md[0:32, :] = act[31 * C :, 0:128]
     md[32:64, :] = act[31 * C :, 128:256]
     md[64:128, :] = pool[192:256, :]
-    low = jnp.zeros((C, 128), F32)
-    high = jnp.zeros((C, 128), F32)
+    low = jnp.zeros((C, 128), BF16)
+    high = jnp.zeros((C, 128), BF16)
     for j in range(8):
         for v in range(4):
             at = (4 * j + v) * C
             t = 8 * j + v
-            low = jnp.where(lane == t, roll(act[at : at + C, 0:128].astype(F32), t), low)
-            high = jnp.where(lane == t, roll(act[at : at + C, 128:256].astype(F32), t - 127), high)
+            low = jnp.where(lane == t, roll(act[at : at + C, 0:128], t), low)
+            high = jnp.where(lane == t, roll(act[at : at + C, 128:256], t - 127), high)
         t = 8 * j + 4
         two = (lane == t) | (lane == t + 1)
-        value = pool[j * C : j * C + C, :].astype(F32)
+        value = pool[j * C : j * C + C, :]
         low = jnp.where(two, roll(value, t - 32), low)
         high = jnp.where(two, roll(value, t - 94), high)
-    el[...] = low.astype(BF16)
-    er[...] = high.astype(BF16)
+    el[...] = low
+    er[...] = high
     edge_copies = start(
         3, ring_plan(mu, md, el, er), [r_m.at[0], r_m.at[1]] + [r_e.at[n] for n in range(6)]
     )
@@ -417,22 +428,22 @@
     for b, ref in enumerate((up0, up1, up2)):
         ref[...] = jnp.dot(parts, spread_mid if b == 1 else spread(b), preferred_element_type=F32)
 
-    tiles = [r_e[n].astype(F32) for n in range(6)]
+    tiles = [r_e[n] for n in range(6)]
     for row in range(-1, R + 1):
         if row < 0:
-            x = jnp.concatenate([r_m[0, 0:32, :], r_m[0, 32:64, :]], axis=1).astype(F32)
+            x = jnp.concatenate([r_m[0, 0:32, :], r_m[0, 32:64, :]], axis=1)
             low, high, t = tiles[2], tiles[3], 59
         elif row == R:
-            x = jnp.concatenate([r_m[1, 0:32, :], r_m[1, 32:64, :]], axis=1).astype(F32)
+            x = jnp.concatenate([r_m[1, 0:32, :], r_m[1, 32:64, :]], axis=1)
             low, high, t = tiles[4], tiles[5], 0
         else:
-            x = act[row * C : row * C + C, :].astype(F32)
+            x = act[row * C : row * C + C, :]
             low, high, t = tiles[0], tiles[1], 8 * (row // 4) + row % 4
         at = ((row + 4) // 4) * C
         back, mid, ahead = with_edges(x, roll(low, -t), roll(high, 127 - t))
-        back = (back + up0[at : at + C, :]) * first_lane
-        mid = mid + up1[at : at + C, :]
-        ahead = (ahead + up2[at : at + C, :]) * last_lane
+        back = (back.astype(F32) + up0[at : at + C, :]) * first_lane
+        mid = mid.astype(F32) + up1[at : at + C, :]
+        ahead = (ahead.astype(F32) + up2[at : at + C, :]) * last_lane
         if row < 0 or row == R:
             keep = has_up if row < 0 else has_down
             back, mid, ahead = back * keep, mid * keep, ahead * keep
@@ -470,9 +481,7 @@
     for k in range(R // B):
         rows = slice(k * B * C, (k + 1) * B * C)
         depth = slice(k * B * 96, k * B * 96 + K)
-        value = jnp.dot(w2[...], b3[depth, :], preferred_element_type=F32)
-        pf[0, rows, :] = value[:, 0:128]
-        pf[1, rows, :] = value[:, 128:256]
+        pf[rows, :] = jnp.dot(w2[...], b3[depth, :], preferred_element_type=F32).astype(BF16)
     arrived(copies)
     total = grad_ref[me]
     for d in range(1, pieces):
@@ -482,9 +491,7 @@
     copies = []
     for d in range(1, nrows):
         copies.append(send_to(in_column(d), mine, column.at[my_row], send_b.at[d], recv_b.at[d]))
-    for o in range(C):
-        for t in range(2):
-            pred_ref[0, o, :, t * 128 : t * 128 + 128] = pf[t, pl.ds(o, R, stride=C), :].astype(BF16)
+    pred_ref[0] = jnp.transpose(pf[...].reshape(R, C, S), (1, 0, 2))
     arrived(copies)
     total = column[0]
     for n in range(1, nrows):
@@ -510,13 +517,13 @@
         return pltpu.VMEM(shape, BF16)
 
     height, nrows = 192 // pieces, lax.axis_size("rows")
-    scratch = [f(2, R * C, 128), f(2, R * C, 128), h(R * C, S), h(R * C, S)]
+    scratch = [h(R * C, S), h(R * C, S)]
     scratch += [h(160, 128), h(160, 128), h(C, 128), h(C, 128)]
-    scratch += [f(4, 66 * C, 128), f(2, (R + 2) * 96, 128)]
+    scratch += [f(4, 72 * PITCH, 128), f(3, (R + 8) * PITCH, 128)]
     scratch += [h((R + 2) * 96, S), h((R + 2) * 96, S)] + [h(B * C, K)] * 5
     scratch += [h(R * C, S), f(R * C, S), h(R * C, S), h(256, 128), h(256, 128)]
     scratch += [h(128, 128), h(128, 128)] + [h(C, 128)] * 4
-    scratch += [h(12 * 96, 128), h((R + 2) * 96, S), h(R * C, S), f(2, R * C, 128)]
+    scratch += [h(12 * 96, 128), h((R + 2) * 96, S), h(R * C, S), h(R * C, S)]
     scratch += [f(10 * C, S)] * 3
     scratch += [h(2, C, S), h(6, C, 128), h(2, 17 * C, S), h(2, 160, 128), h(4, 96, 128)]
     scratch += [h(2, C, 128), h(6, C, 128), h(2, 128, 128), h(6, C, 128)]

time: 60.2 us -> 56.5 us (0.939)
  Pallas kernels: 59.4 us -> 55.8 us
    pallas_call x1, Pallas kernels: 57.4 us -> 53.8 us  [main(): pl.pallas_call(functools.partial(main_kernel, factor), out_shape=(jax.Sha...]
where the time goes in v4:
time: 56.5 us; the launch traced here: 56.4 us
  Pallas kernels  55.8 us (99%)
  between operations  0.64 us (1%)
    pallas_call x1, Pallas kernels, main(): pl.pallas_call(functools.partial(main_kernel, factor), out_shape=(jax.Sha...  53.8 us
    pallas_call x1, Pallas kernels, finish(): pl.pallas_call(finish_kernel, out_shape=(jax.ShapeDtypeStruct(prediction....  2 us

profile of v4, /device:TPU:1, one launch (start us, length us, event | category | flops | bytes accessed | tf_op | source)
XLA Modules:
  0.0 56.4 jit_solution(6082442014938092257)
XLA Ops:
  0.6 53.8 %main.1 = (bf16[1,32,32,256]{3,2,1,0:T(8,128)(2,1)}, f32[16,12,128]{2,1,0:T(8,128)}) custom-call(bf16[1,32,32,256]{3,2,1,0:T(8,128)(2,1)} %feat_ref.1, bf16[1,32,32,256]{3,2,1,0:T(8,128)(2,1)} %cot_ref.1, s32[1,2,32]{2,1,0:T(2,128)} %bitcast.1, bf16[9,32,32]{2,1,0:T(8,128)(2,1)} %k1_ref.1, bf16[9,32,32]{2,1,0:T(8,128)(2,1)} %kb_ref.1, bf16[9,32,32]{2,1,0:T(8,128)(2,1)} %k2_ref.1), custom_call_target="tpu_custom_call" | custom-call | tf_op jit(solution)/shard_map/main/pallas_call | solution.py:535
  54.4 2.0 %finish.1 = (bf16[1,32,32,256]{3,2,1,0:T(8,128)(2,1)}, f32[9,32,32]{2,1,0:T(8,128)}, f32[9,32,32]{2,1,0:T(8,128)}) custom-call(bf16[1,32,32,256]{3,2,1,0:T(8,128)(2,1)} %get-tuple-element.5.pred_ref, f32[16,12,128]{2,1,0:T(8,128)} %get-tuple-element.6.sums_ref), custom_call_target="tpu_custom_call" | custom-call | tf_op jit(solution)/shard_map/finish/pallas_call | solution.py:559

commit v5 on v4

--- a/solution.py
+++ b/solution.py
@@ -127,32 +127,53 @@
 
 def main_kernel(
     factor,
-    feat_ref, cot_ref, shift_ref, k1_ref, kb_ref, k2_ref,
-    pred_ref, out_ref,
+    feat_hbm, cot_hbm, shift_hbm, k1_hbm, kb_hbm, k2_hbm,
+    pred_hbm, out_ref,
+    feat_ref, cot_ref, shift_ref, k1_ref, kb_ref, k2_ref, pred_ref,
     ft, ct, sl, sr, cl, cr, fe, xf, x3, c3, w1, w2, w2t, wb, wbt,
     act, slope, bg, pool, coarse, mu, md, el, er, gl, gr, p3, b3, pg, pf, up0, up1, up2,
     r_cot_row, r_cot_tile, r_row, r_strip, r_corner, r_gc_row, r_gc_tile, r_m, r_e,
-    grad_ref, held, mine, column,
-    send, recv, send_a, recv_a, send_b, recv_b, send_c, recv_c,
+    grad_ref, held, mine, mine_y, sums_y, sums_z,
+    load_sem, store_sem, send, recv, send_a, recv_a, send_y, recv_y, send_z, recv_z, send_c, recv_c,
 ):
     device = neighbours()
     my_row, col, img = lax.axis_index("rows"), lax.axis_index("cols"), lax.axis_index("dp")
     nrows, ncols, ndp = lax.axis_size("rows"), lax.axis_size("cols"), lax.axis_size("dp")
-    pieces = ncols * ndp
-    me = col * ndp + img
-
-    def peer(d):
+    depth_z, pieces = nrows // 2, ncols // 2 * ndp
+    my_x, my_high, my_low, my_z = col // 2, lax.rem(col, 2), my_row // depth_z, lax.rem(my_row, depth_z)
+    me = my_x * ndp + img
+    my_y = my_high * 2 + my_low
+
+    def near(d):
         other = lax.rem(me + d, pieces)
-        return other, {"cols": other // ndp, "dp": lax.rem(other, ndp)}
-
-    def in_column(d):
-        return {"rows": lax.rem(my_row + d, nrows)}
+        return other, {"cols": other // ndp * 2 + my_high, "dp": lax.rem(other, ndp)}
+
+    def along_y(d):
+        other = lax.rem(my_y + d, 4)
+        return {"cols": my_x * 2 + other // 2, "rows": lax.rem(other, 2) * depth_z + my_z}
+
+    def along_z(d):
+        return {"rows": my_low * depth_z + lax.rem(my_z + d, depth_z)}
 
     barrier = pltpu.get_barrier_semaphore()
-    greeted = [device(dr, dc) for dr in (-1, 1) for dc in (-1, 1)]
-    greeted += [in_column(d) for d in range(1, nrows)] + [peer(d)[1] for d in range(1, pieces)]
+    greeted = [device(dr, dc) for dr in (-1, 0, 1) for dc in (-1, 0, 1) if dr or dc]
+    greeted += [along_z(d) for d in range(1, depth_z)] + [along_y(d) for d in range(1, 4)]
+    greeted += [near(d)[1] for d in range(1, pieces)]
     for other in greeted:
         pl.semaphore_signal(barrier, inc=1, device_id=other, device_id_type=MESH)
+    loads = []
+    for n, (source, target) in enumerate(
+        (
+            (cot_hbm, cot_ref),
+            (feat_hbm, feat_ref),
+            (k2_hbm, k2_ref),
+            (k1_hbm, k1_ref),
+            (kb_hbm, kb_ref),
+            (shift_hbm, shift_ref),
+        )
+    ):
+        loads.append(pltpu.make_async_copy(source, target, load_sem.at[n]))
+        loads[-1].start()
     has_up, has_down, has_left, has_right = edge_flags()
     started = []
 
@@ -178,6 +199,7 @@
             copy.wait_recv()
 
     lane = lanes((C, 128))
+    loads[0].wait()
     ct[...] = jnp.transpose(cot_ref[0], (1, 0, 2)).reshape(R * C, S)
     low = jnp.zeros((C, 128), BF16)
     high = jnp.zeros((C, 128), BF16)
@@ -187,6 +209,7 @@
         high = jnp.where(lane == r, roll(ct[at, 128:256], r - 127), high)
     cl[...] = low
     cr[...] = high
+    loads[1].wait()
     ft[...] = jnp.transpose(feat_ref[0], (1, 0, 2)).reshape(R * C, S)
     for p in range(5):
         low = jnp.zeros((C, 128), BF16)
@@ -221,6 +244,8 @@
         [r_row.at[0], r_row.at[1], r_strip.at[0], r_strip.at[1]] + [r_corner.at[n] for n in range(4)],
     )
 
+    for copy in loads[2:]:
+        copy.wait()
     w2t[...] = banded(backward_taps(k2_ref))
     w1[...] = banded(forward_taps(k1_ref))
     wbt[...] = banded(backward_taps(kb_ref))
@@ -476,7 +501,7 @@
 
     copies = []
     for d in range(1, pieces):
-        other, device_id = peer(d)
+        other, device_id = near(d)
         copies.append(send_to(device_id, grad_ref.at[other], held.at[d], send_a.at[d], recv_a.at[d]))
     for k in range(R // B):
         rows = slice(k * B * C, (k + 1) * B * C)
@@ -487,20 +512,30 @@
     for d in range(1, pieces):
         total = total + held[d]
     mine[...] = total
-    column[my_row] = total
+    sums_y[my_y] = total
     copies = []
-    for d in range(1, nrows):
-        copies.append(send_to(in_column(d), mine, column.at[my_row], send_b.at[d], recv_b.at[d]))
+    for d in range(1, 4):
+        copies.append(send_to(along_y(d), mine, sums_y.at[my_y], send_y.at[d], recv_y.at[d]))
     pred_ref[0] = jnp.transpose(pf[...].reshape(R, C, S), (1, 0, 2))
+    store = pltpu.make_async_copy(pred_ref, pred_hbm, store_sem)
+    store.start()
     arrived(copies)
-    total = column[0]
-    for n in range(1, nrows):
-        total = total + column[n]
+    total = (sums_y[0] + sums_y[1]) + (sums_y[2] + sums_y[3])
+    mine_y[...] = total
+    sums_z[my_z] = total
+    copies = []
+    for d in range(1, depth_z):
+        copies.append(send_to(along_z(d), mine_y, sums_z.at[my_z], send_z.at[d], recv_z.at[d]))
+    arrived(copies)
+    total = sums_z[0]
+    for n in range(1, depth_z):
+        total = total + sums_z[n]
     out_ref[me] = total
     copies = []
     for d in range(1, pieces):
-        copies.append(send_to(peer(d)[1], out_ref.at[me], out_ref.at[me], send_c.at[d], recv_c.at[d]))
+        copies.append(send_to(near(d)[1], out_ref.at[me], out_ref.at[me], send_c.at[d], recv_c.at[d]))
     arrived(copies)
+    store.wait()
     for copy in started:
         copy.wait_send()
 
@@ -517,7 +552,10 @@
         return pltpu.VMEM(shape, BF16)
 
     height, nrows = 192 // pieces, lax.axis_size("rows")
-    scratch = [h(R * C, S), h(R * C, S)]
+    depth_z = nrows // 2
+    scratch = [h(1, C, R, S), h(1, C, R, S), pltpu.SMEM((1, 2, C), jnp.int32)]
+    scratch += [h(9, C, C)] * 3 + [h(1, C, R, S)]
+    scratch += [h(R * C, S), h(R * C, S)]
     scratch += [h(160, 128), h(160, 128), h(C, 128), h(C, 128)]
     scratch += [f(4, 72 * PITCH, 128), f(3, (R + 8) * PITCH, 128)]
     scratch += [h((R + 2) * 96, S), h((R + 2) * 96, S)] + [h(B * C, K)] * 5
@@ -527,41 +565,59 @@
     scratch += [f(10 * C, S)] * 3
     scratch += [h(2, C, S), h(6, C, 128), h(2, 17 * C, S), h(2, 160, 128), h(4, 96, 128)]
     scratch += [h(2, C, 128), h(6, C, 128), h(2, 128, 128), h(6, C, 128)]
-    scratch += [f(pieces, height, 128), f(pieces, height, 128), f(height, 128), f(nrows, height, 128)]
+    scratch += [f(pieces, height, 128), f(pieces, height, 128), f(height, 128), f(height, 128)]
+    scratch += [f(4, height, 128), f(depth_z, height, 128), pltpu.SemaphoreType.DMA((6,)), pltpu.SemaphoreType.DMA]
     scratch += [pltpu.SemaphoreType.DMA((4, 8)), pltpu.SemaphoreType.DMA((4, 8))]
-    scratch += [pltpu.SemaphoreType.DMA((n,)) for n in (pieces, pieces, nrows, nrows, pieces, pieces)]
-    specs = vmem(6)
-    specs[2] = pl.BlockSpec(memory_space=pltpu.SMEM)
+    scratch += [pltpu.SemaphoreType.DMA((n,)) for n in (pieces, pieces, 4, 4, depth_z, depth_z, pieces, pieces)]
+    hbm = pl.BlockSpec(memory_space=pl.ANY)
     return pl.pallas_call(
         functools.partial(main_kernel, factor),
         out_shape=(
             jax.ShapeDtypeStruct((1, C, R, S), BF16),
             jax.ShapeDtypeStruct((pieces, 192 // pieces, 128), F32),
         ),
-        in_specs=specs,
-        out_specs=tuple(vmem(2)),
+        in_specs=[hbm] * 6,
+        out_specs=(hbm, vmem(1)[0]),
         scratch_shapes=scratch,
         compiler_params=pltpu.CompilerParams(collective_id=0, has_side_effects=True),
         name="main",
     )(features, cotangent, shifts, k1, kb, k2)
 
 
-def finish_kernel(pred_ref, sums_ref, out_ref, first_ref, second_ref):
-    out_ref[...] = pred_ref[...]
+def finish_kernel(pred_ref, sums_ref, out_ref, first_ref, second_ref, held, sem_in, sem_out):
+    parts = 4
+    size = C // parts
+    loads, stores = [], []
+    for n in range(parts):
+        at = slice(n * size, n * size + size)
+        loads.append(pltpu.make_async_copy(pred_ref.at[0, at], held.at[at], sem_in.at[n]))
+        stores.append(pltpu.make_async_copy(held.at[at], out_ref.at[0, at], sem_out.at[n]))
+        loads[n].start()
+    for n in range(parts):
+        loads[n].wait()
+        stores[n].start()
     whole = jnp.concatenate([sums_ref[n] for n in range(sums_ref.shape[0])], axis=0)
     for t in range(9):
         for n, ref in enumerate((first_ref, second_ref)):
             at = (t // 4) * 64 + n * C
             ref[t] = roll(whole[at : at + C, :], -32 * (t % 4))[:, 0:C]
+    for n in range(parts):
+        stores[n].wait()
 
 
 def finish(prediction, sums):
+    hbm = pl.BlockSpec(memory_space=pl.ANY)
     return pl.pallas_call(
         finish_kernel,
         out_shape=(jax.ShapeDtypeStruct(prediction.shape, BF16),)
         + (jax.ShapeDtypeStruct((9, C, C), F32),) * 2,
-        in_specs=vmem(2),
-        out_specs=tuple(vmem(3)),
+        in_specs=[hbm] + vmem(1),
+        out_specs=(hbm,) + tuple(vmem(2)),
+        scratch_shapes=[
+            pltpu.VMEM((C, R, S), BF16),
+            pltpu.SemaphoreType.DMA((4,)),
+            pltpu.SemaphoreType.DMA((4,)),
+        ],
         name="finish",
     )(prediction, sums)
 
@@ -571,7 +627,7 @@
     assert features.shape == (1, C, R, S)
     factor = 1.0 / math.sqrt(ndp * nrows * R * ncols * S)
     prediction, grads = main(
-        factor, ncols * ndp, features, cotangent, shifts.transpose(0, 2, 1), first_kernel, bottle_kernel, second_kernel
+        factor, ncols // 2 * ndp, features, cotangent, shifts.transpose(0, 2, 1), first_kernel, bottle_kernel, second_kernel
     )
     return finish(prediction, grads)
 

time: 56.5 us -> 55.7 us (0.986)
  Pallas kernels: 55.8 us -> 54.9 us
    pallas_call x1, Pallas kernels: 53.8 us -> 51.5 us  [main(): pl.pallas_call(functools.partial(main_kernel, factor), out_shape=(jax.Sha...]
    pallas_call x1, Pallas kernels: 2 us -> 3.42 us  [finish(): pl.pallas_call(finish_kernel, out_shape=(jax.ShapeDtypeStruct(prediction....]
where the time goes in v5:
time: 55.7 us; the launch traced here: 55.5 us
  Pallas kernels  54.9 us (99%)
  between operations  0.64 us (1%)
    pallas_call x1, Pallas kernels, main(): pl.pallas_call(functools.partial(main_kernel, factor), out_shape=(jax.Sha...  51.5 us
    pallas_call x1, Pallas kernels, finish(): pl.pallas_call(finish_kernel, out_shape=(jax.ShapeDtypeStruct(prediction....  3.42 us

profile of v5, /device:TPU:1, one launch (start us, length us, event | category | flops | bytes accessed | tf_op | source)
XLA Modules:
  0.0 55.5 jit_solution(11798422074740449208)
XLA Ops:
  0.6 51.5 %main.1 = (bf16[1,32,32,256]{3,2,1,0:T(8,128)(2,1)}, f32[8,24,128]{2,1,0:T(8,128)}) custom-call(bf16[1,32,32,256]{3,2,1,0:T(8,128)(2,1)} %feat_hbm.1, bf16[1,32,32,256]{3,2,1,0:T(8,128)(2,1)} %cot_hbm.1, s32[1,2,32]{2,1,0:T(2,128)} %bitcast.1, bf16[9,32,32]{2,1,0:T(8,128)(2,1)} %k1_hbm.1, bf16[9,32,32]{2,1,0:T(8,128)(2,1)} %kb_hbm.1, bf16[9,32,32]{2,1,0:T(8,128)(2,1)} %k2_hbm.1), custom_call_target="tpu_custom_call" | custom-call | tf_op jit(solution)/shard_map/main/pallas_call | solution.py:573
  52.1 3.4 %finish.1 = (bf16[1,32,32,256]{3,2,1,0:T(8,128)(2,1)}, f32[9,32,32]{2,1,0:T(8,128)}, f32[9,32,32]{2,1,0:T(8,128)}) custom-call(bf16[1,32,32,256]{3,2,1,0:T(8,128)(2,1)} %get-tuple-element.5.pred_ref, f32[8,24,128]{2,1,0:T(8,128)} %get-tuple-element.6.sums_ref), custom_call_target="tpu_custom_call" | custom-call | tf_op jit(solution)/shard_map/finish/pallas_call | solution.py:610

commit v6 on v5

--- a/solution.py
+++ b/solution.py
@@ -106,14 +106,14 @@
 
 def ring_plan(up, down, left, right, left_up=None, left_down=None, right_up=None, right_down=None):
     return (
-        (1, 0, down, 0),
-        (-1, 0, up, 1),
-        (0, 1, right, 2),
-        (0, -1, left, 3),
         (1, 1, right if right_down is None else right_down, 4),
         (1, -1, left if left_down is None else left_down, 5),
         (-1, 1, right if right_up is None else right_up, 6),
         (-1, -1, left if left_up is None else left_up, 7),
+        (0, 1, right, 2),
+        (0, -1, left, 3),
+        (1, 0, down, 0),
+        (-1, 0, up, 1),
     )
 
 
@@ -584,40 +584,22 @@
     )(features, cotangent, shifts, k1, kb, k2)
 
 
-def finish_kernel(pred_ref, sums_ref, out_ref, first_ref, second_ref, held, sem_in, sem_out):
-    parts = 4
-    size = C // parts
-    loads, stores = [], []
-    for n in range(parts):
-        at = slice(n * size, n * size + size)
-        loads.append(pltpu.make_async_copy(pred_ref.at[0, at], held.at[at], sem_in.at[n]))
-        stores.append(pltpu.make_async_copy(held.at[at], out_ref.at[0, at], sem_out.at[n]))
-        loads[n].start()
-    for n in range(parts):
-        loads[n].wait()
-        stores[n].start()
+def finish_kernel(pred_ref, sums_ref, out_ref, first_ref, second_ref):
+    out_ref[...] = pred_ref[...]
     whole = jnp.concatenate([sums_ref[n] for n in range(sums_ref.shape[0])], axis=0)
     for t in range(9):
         for n, ref in enumerate((first_ref, second_ref)):
             at = (t // 4) * 64 + n * C
             ref[t] = roll(whole[at : at + C, :], -32 * (t % 4))[:, 0:C]
-    for n in range(parts):
-        stores[n].wait()
 
 
 def finish(prediction, sums):
-    hbm = pl.BlockSpec(memory_space=pl.ANY)
     return pl.pallas_call(
         finish_kernel,
         out_shape=(jax.ShapeDtypeStruct(prediction.shape, BF16),)
         + (jax.ShapeDtypeStruct((9, C, C), F32),) * 2,
-        in_specs=[hbm] + vmem(1),
-        out_specs=(hbm,) + tuple(vmem(2)),
-        scratch_shapes=[
-            pltpu.VMEM((C, R, S), BF16),
-            pltpu.SemaphoreType.DMA((4,)),
-            pltpu.SemaphoreType.DMA((4,)),
-        ],
+        in_specs=vmem(2),
+        out_specs=tuple(vmem(3)),
         name="finish",
     )(prediction, sums)
 

time: 55.7 us -> 53.4 us (0.959)
  Pallas kernels: 54.9 us -> 52.6 us
    pallas_call x1, Pallas kernels: 3.42 us -> 1.99 us  [finish(): pl.pallas_call(finish_kernel, out_shape=(jax.ShapeDtypeStruct(prediction....]
    pallas_call x1, Pallas kernels: 51.5 us -> 50.6 us  [main(): pl.pallas_call(functools.partial(main_kernel, factor), out_shape=(jax.Sha...]
where the time goes in v6:
time: 53.4 us; the launch traced here: 53.2 us
  Pallas kernels  52.6 us (99%)
  between operations  0.64 us (1%)
    pallas_call x1, Pallas kernels, main(): pl.pallas_call(functools.partial(main_kernel, factor), out_shape=(jax.Sha...  50.6 us
    pallas_call x1, Pallas kernels, finish(): pl.pallas_call(finish_kernel, out_shape=(jax.ShapeDtypeStruct(prediction....  1.99 us

profile of v6, /device:TPU:1, one launch (start us, length us, event | category | flops | bytes accessed | tf_op | source)
XLA Modules:
  0.0 53.2 jit_solution(8114345959572911295)
XLA Ops:
  0.6 50.6 %main.1 = (bf16[1,32,32,256]{3,2,1,0:T(8,128)(2,1)}, f32[8,24,128]{2,1,0:T(8,128)}) custom-call(bf16[1,32,32,256]{3,2,1,0:T(8,128)(2,1)} %feat_hbm.1, bf16[1,32,32,256]{3,2,1,0:T(8,128)(2,1)} %cot_hbm.1, s32[1,2,32]{2,1,0:T(2,128)} %bitcast.1, bf16[9,32,32]{2,1,0:T(8,128)(2,1)} %k1_hbm.1, bf16[9,32,32]{2,1,0:T(8,128)(2,1)} %kb_hbm.1, bf16[9,32,32]{2,1,0:T(8,128)(2,1)} %k2_hbm.1), custom_call_target="tpu_custom_call" | custom-call | tf_op jit(solution)/shard_map/main/pallas_call | solution.py:573
  51.2 2.0 %finish.1 = (bf16[1,32,32,256]{3,2,1,0:T(8,128)(2,1)}, f32[9,32,32]{2,1,0:T(8,128)}, f32[9,32,32]{2,1,0:T(8,128)}) custom-call(bf16[1,32,32,256]{3,2,1,0:T(8,128)(2,1)} %get-tuple-element.5.pred_ref, f32[8,24,128]{2,1,0:T(8,128)} %get-tuple-element.6.sums_ref), custom_call_target="tpu_custom_call" | custom-call | tf_op jit(solution)/shard_map/finish/pallas_call | solution.py:597

commit v7 on v6

--- a/solution.py
+++ b/solution.py
@@ -130,9 +130,9 @@
     feat_hbm, cot_hbm, shift_hbm, k1_hbm, kb_hbm, k2_hbm,
     pred_hbm, out_ref,
     feat_ref, cot_ref, shift_ref, k1_ref, kb_ref, k2_ref, pred_ref,
-    ft, ct, sl, sr, cl, cr, fe, xf, x3, c3, w1, w2, w2t, wb, wbt,
+    ft, ct, sl, sr, fe, xf, x3, c3, w1, w2, w2t, wb, wbt,
     act, slope, bg, pool, coarse, mu, md, el, er, gl, gr, p3, b3, pg, pf, up0, up1, up2,
-    r_cot_row, r_cot_tile, r_row, r_strip, r_corner, r_gc_row, r_gc_tile, r_m, r_e,
+    r_cot_row, r_row, r_strip, r_corner, r_gc_row, r_gc_tile, r_m, r_e,
     grad_ref, held, mine, mine_y, sums_y, sums_z,
     load_sem, store_sem, send, recv, send_a, recv_a, send_y, recv_y, send_z, recv_z, send_c, recv_c,
 ):
@@ -194,6 +194,11 @@
         started.extend(copies)
         return copies
 
+    def settle():
+        for copy in started:
+            copy.wait_send()
+        started.clear()
+
     def arrived(copies):
         for copy in copies:
             copy.wait_recv()
@@ -201,14 +206,6 @@
     lane = lanes((C, 128))
     loads[0].wait()
     ct[...] = jnp.transpose(cot_ref[0], (1, 0, 2)).reshape(R * C, S)
-    low = jnp.zeros((C, 128), BF16)
-    high = jnp.zeros((C, 128), BF16)
-    for r in range(R):
-        at = slice(r * C, r * C + C)
-        low = jnp.where(lane == r, roll(ct[at, 0:128], r), low)
-        high = jnp.where(lane == r, roll(ct[at, 128:256], r - 127), high)
-    cl[...] = low
-    cr[...] = high
     loads[1].wait()
     ft[...] = jnp.transpose(feat_ref[0], (1, 0, 2)).reshape(R * C, S)
     for p in range(5):
@@ -221,13 +218,16 @@
                 here = (lane >= 18 * g) & (lane < 18 * g + 17)
                 low = jnp.where(here, roll(ft[at, 0:128], 18 * g), low)
                 high = jnp.where(here, roll(ft[at, 128:256], 18 * g + 17), high)
+                spare = 18 * g + 17
+                low = jnp.where(lane == spare, roll(ct[at, 0:128], spare), low)
+                high = jnp.where(lane == spare, roll(ct[at, 128:256], spare - 127), high)
         sl[p * C : p * C + C, :] = low
         sr[p * C : p * C + C, :] = high
     pl.semaphore_wait(barrier, len(greeted))
     cot_copies = start(
         0,
-        ring_plan(ct.at[0:C, :], ct.at[(R - 1) * C : R * C, :], cl, cr),
-        [r_cot_row.at[0], r_cot_row.at[1]] + [r_cot_tile.at[n] for n in range(6)],
+        ring_plan(ct.at[0:C, :], ct.at[(R - 1) * C : R * C, :], None, None)[6:],
+        [r_cot_row.at[0], r_cot_row.at[1]],
     )
     feat_copies = start(
         1,
@@ -266,24 +266,31 @@
             at = (2 * k + j) * C
             ref[at : at + C, :] = (four * scale).astype(BF16)
 
-    arrived(cot_copies)
-    tiles = [r_cot_tile[n] for n in range(6)]
+    for r in range(R):
+        x = ct[r * C : r * C + C, :]
+        store_three(c3, r + 1, (roll(x, 1), x, roll(x, S - 1)))
+
+    arrived(cot_copies + feat_copies[:6])
     left_flag, right_flag = has_left.astype(BF16), has_right.astype(BF16)
     up_flag, down_flag = has_up.astype(BF16), has_down.astype(BF16)
     for r in range(-1, R + 1):
         if r < 0:
             x = r_cot_row[0] * up_flag
-            a, b, t, keep = tiles[2], tiles[3], R - 1, up_flag
+            a, b, t, keep = r_corner[0, 64:96, :], r_corner[1, 64:96, :], 3, up_flag
         elif r == R:
             x = r_cot_row[1] * down_flag
-            a, b, t, keep = tiles[4], tiles[5], 0, down_flag
+            a, b, t, keep = r_corner[2, 0:32, :], r_corner[3, 0:32, :], 0, down_flag
         else:
-            x = ct[r * C : r * C + C, :]
-            a, b, t, keep = tiles[0], tiles[1], r, None
-        a, b = roll(a, -t) * left_flag, roll(b, 127 - t) * right_flag
-        if keep is not None:
-            a, b = a * keep, b * keep
-        store_three(c3, r + 1, with_edges(x, a, b))
+            at = (r // 7) * C
+            a, b, t, keep = r_strip[0, at : at + C, :], r_strip[1, at : at + C, :], r % 7, None
+        a, b = roll(a, -(18 * t + 17)) * left_flag, roll(b, 110 - 18 * t) * right_flag
+        if keep is None:
+            at = (r + 1) * 96
+            c3[at : at + C, 0:128] = jnp.where(lane == 0, a, c3[at : at + C, 0:128])
+            at += 2 * C
+            c3[at : at + C, 128:256] = jnp.where(lane == 127, b, c3[at : at + C, 128:256])
+        else:
+            store_three(c3, r + 1, with_edges(x, a * keep, b * keep))
     for k in range(R // B):
         rows = slice(k * B * C, (k + 1) * B * C)
         depth = slice(k * B * 96, k * B * 96 + K)
@@ -304,7 +311,7 @@
         [r_gc_row.at[0], r_gc_row.at[1]] + [r_gc_tile.at[n] for n in range(6)],
     )
 
-    arrived(feat_copies)
+    arrived(feat_copies[6:])
     for t in range(2):
         cols = slice(t * 128, t * 128 + 128)
         for r in range(17):
@@ -346,9 +353,6 @@
             jnp.where(after, turned[1], turned[0]),
             jnp.where(before, turned[2], turned[3]),
         )
-    wide = lanes((C, S))
-    first_lane = jnp.where(wide == 0, has_left, 1.0)
-    last_lane = jnp.where(wide == S - 1, has_right, 1.0)
     edge_lane = jnp.where(lane >= 64, has_left, has_right)
     for row in range(R + 2):
         at = slice(row * PITCH, row * PITCH + C)
@@ -440,6 +444,9 @@
         total = part if total is None else total + part
     first = collected(total, factor)
 
+    spreads = (spread(0), spread_mid, spread(2))
+    first_lane = jnp.where(lanes((1, S)) == 0, has_left, 1.0)
+    last_lane = jnp.where(lanes((1, S)) == S - 1, has_right, 1.0)
     arrived(edge_copies)
     cells(2, pooled_row, r_e, lambda j: 8 * j + 4)
     bottle = jnp.concatenate(
@@ -451,9 +458,10 @@
     )
     parts = halves(bottle)
     for b, ref in enumerate((up0, up1, up2)):
-        ref[...] = jnp.dot(parts, spread_mid if b == 1 else spread(b), preferred_element_type=F32)
-
-    tiles = [r_e[n] for n in range(6)]
+        value = jnp.dot(parts, spreads[b], preferred_element_type=F32)
+        ref[...] = value if b == 1 else value * (first_lane if b == 0 else last_lane)
+
+    tiles = [r_e[n] * (right_flag if n % 2 else left_flag) for n in range(6)]
     for row in range(-1, R + 1):
         if row < 0:
             x = jnp.concatenate([r_m[0, 0:32, :], r_m[0, 32:64, :]], axis=1)
@@ -466,9 +474,9 @@
             low, high, t = tiles[0], tiles[1], 8 * (row // 4) + row % 4
         at = ((row + 4) // 4) * C
         back, mid, ahead = with_edges(x, roll(low, -t), roll(high, 127 - t))
-        back = (back.astype(F32) + up0[at : at + C, :]) * first_lane
+        back = back.astype(F32) + up0[at : at + C, :]
         mid = mid.astype(F32) + up1[at : at + C, :]
-        ahead = (ahead.astype(F32) + up2[at : at + C, :]) * last_lane
+        ahead = ahead.astype(F32) + up2[at : at + C, :]
         if row < 0 or row == R:
             keep = has_up if row < 0 else has_down
             back, mid, ahead = back * keep, mid * keep, ahead * keep
@@ -519,6 +527,7 @@
     pred_ref[0] = jnp.transpose(pf[...].reshape(R, C, S), (1, 0, 2))
     store = pltpu.make_async_copy(pred_ref, pred_hbm, store_sem)
     store.start()
+    settle()
     arrived(copies)
     total = (sums_y[0] + sums_y[1]) + (sums_y[2] + sums_y[3])
     mine_y[...] = total
@@ -526,6 +535,7 @@
     copies = []
     for d in range(1, depth_z):
         copies.append(send_to(along_z(d), mine_y, sums_z.at[my_z], send_z.at[d], recv_z.at[d]))
+    store.wait()
     arrived(copies)
     total = sums_z[0]
     for n in range(1, depth_z):
@@ -534,10 +544,8 @@
     copies = []
     for d in range(1, pieces):
         copies.append(send_to(near(d)[1], out_ref.at[me], out_ref.at[me], send_c.at[d], recv_c.at[d]))
+    settle()
     arrived(copies)
-    store.wait()
-    for copy in started:
-        copy.wait_send()
 
 
 def vmem(n):
@@ -556,14 +564,14 @@
     scratch = [h(1, C, R, S), h(1, C, R, S), pltpu.SMEM((1, 2, C), jnp.int32)]
     scratch += [h(9, C, C)] * 3 + [h(1, C, R, S)]
     scratch += [h(R * C, S), h(R * C, S)]
-    scratch += [h(160, 128), h(160, 128), h(C, 128), h(C, 128)]
+    scratch += [h(160, 128), h(160, 128)]
     scratch += [f(4, 72 * PITCH, 128), f(3, (R + 8) * PITCH, 128)]
     scratch += [h((R + 2) * 96, S), h((R + 2) * 96, S)] + [h(B * C, K)] * 5
     scratch += [h(R * C, S), f(R * C, S), h(R * C, S), h(256, 128), h(256, 128)]
     scratch += [h(128, 128), h(128, 128)] + [h(C, 128)] * 4
     scratch += [h(12 * 96, 128), h((R + 2) * 96, S), h(R * C, S), h(R * C, S)]
     scratch += [f(10 * C, S)] * 3
-    scratch += [h(2, C, S), h(6, C, 128), h(2, 17 * C, S), h(2, 160, 128), h(4, 96, 128)]
+    scratch += [h(2, C, S), h(2, 17 * C, S), h(2, 160, 128), h(4, 96, 128)]
     scratch += [h(2, C, 128), h(6, C, 128), h(2, 128, 128), h(6, C, 128)]
     scratch += [f(pieces, height, 128), f(pieces, height, 128), f(height, 128), f(height, 128)]
     scratch += [f(4, height, 128), f(depth_z, height, 128), pltpu.SemaphoreType.DMA((6,)), pltpu.SemaphoreType.DMA]

time: 53.4 us -> 53 us (level)
  no operation moved by 1% of the time
where the time goes in v7:
time: 53 us; the launch traced here: 52.9 us
  Pallas kernels  52.2 us (98%)
  between operations  0.64 us (1%)
    pallas_call x1, Pallas kernels, main(): pl.pallas_call(functools.partial(main_kernel, factor), out_shape=(jax.Sha...  50.3 us
    pallas_call x1, Pallas kernels, finish(): pl.pallas_call(finish_kernel, out_shape=(jax.ShapeDtypeStruct(prediction....  1.99 us

profile of v7, /device:TPU:1, one launch (start us, length us, event | category | flops | bytes accessed | tf_op | source)
XLA Modules:
  0.0 52.9 jit_solution(12595616688523061316)
XLA Ops:
  0.6 50.3 %main.1 = (bf16[1,32,32,256]{3,2,1,0:T(8,128)(2,1)}, f32[8,24,128]{2,1,0:T(8,128)}) custom-call(bf16[1,32,32,256]{3,2,1,0:T(8,128)(2,1)} %feat_hbm.1, bf16[1,32,32,256]{3,2,1,0:T(8,128)(2,1)} %cot_hbm.1, s32[1,2,32]{2,1,0:T(2,128)} %bitcast.1, bf16[9,32,32]{2,1,0:T(8,128)(2,1)} %k1_hbm.1, bf16[9,32,32]{2,1,0:T(8,128)(2,1)} %kb_hbm.1, bf16[9,32,32]{2,1,0:T(8,128)(2,1)} %k2_hbm.1), custom_call_target="tpu_custom_call" | custom-call | tf_op jit(solution)/shard_map/main/pallas_call | solution.py:581
  50.9 2.0 %finish.1 = (bf16[1,32,32,256]{3,2,1,0:T(8,128)(2,1)}, f32[9,32,32]{2,1,0:T(8,128)}, f32[9,32,32]{2,1,0:T(8,128)}) custom-call(bf16[1,32,32,256]{3,2,1,0:T(8,128)(2,1)} %get-tuple-element.5.pred_ref, f32[8,24,128]{2,1,0:T(8,128)} %get-tuple-element.6.sums_ref), custom_call_target="tpu_custom_call" | custom-call | tf_op jit(solution)/shard_map/finish/pallas_call | solution.py:605
